TPU v7x, 128 devices: a whole 4x4x4 slice. The times are simulated.
128 devices in a mesh: row: 8 (over x, core), col: 16 (over y, z).
Axes of the slice: x: 4, y: 4, z: 4, core: 2. Of those that a mesh axis runs over, the one named last changes fastest.
Arguments:
- coarse_in: bfloat16 [256, 256, 512], P('row', 'col'), may hold values from -6 to 6
- coarse_weight: bfloat16 [27, 64, 64], replicated, may hold values from -0.15625 to 0.15625
- coarse_bias: float32 [64], replicated, may hold values from -3 to 3
- fine_in: bfloat16 [1024, 32768], P(('row', 'col')), may hold values from -6 to 6
- weight_first: bfloat16 [27, 64, 64], replicated, may hold values from -0.15625 to 0.15625
- bias_first: float32 [64], replicated, may hold values from -3 to 3
- weight_second: bfloat16 [27, 64, 64], replicated, may hold values from -0.15625 to 0.15625
- bias_second: float32 [64], replicated, may hold values from -3 to 3
- parent_tile: int32 [1024, 1], P(('row', 'col')), may hold values from 0 to 15; in each aligned block of 8 rows (0 to 7, 8 to 15, ...) at most 2 rows name the same one
- parent_cell: int32 [1024], P(('row', 'col')), may hold values from 0 to 63
- neighbours: int32 [1024, 6], P(('row', 'col')), may hold values from -1 to 1023, as said below
Outputs:
- coarse_out: bfloat16 [256, 256, 512], P('row', 'col')
- fine_out: bfloat16 [1024, 32768], P(('row', 'col'))
Inputs may be any that keep to these rules, and one draw needn't show every extreme that they name: neighbours[g, f] is the block across face f of block g (f = 0..5: -x, +x, -y, +y, -z, +z), or -1; the relation is symmetric: if h is across face f of g, g is across the opposite face of h. Blocks of device d are rows d * 8 to d * 8 + 7, devices numbered row-major over (row, col). A block across a z face lies on the same device; across an x face on the same device or on the device of the adjacent row on that side, same col; across a y face on the same device or on the device of the adjacent col on that side, same row. Between a device and each such neighbouring device at most 8 block pairs are linked, and in every draw some pair along row and some pair along col link exactly 8. `parent_tile`: among the 8 blocks of one device at most 2 have their parents in one tile; some device has exactly 2 in some tile.
All inputs are finite; a program needn't handle non-finite values.
Results may differ from a plain program's by a relative error of at most 0.0057.
Values may be sent and summed in bfloat16 or wider, within the bound.
A program may use at most 128 MiB of HBM per device.

v0:
```python
import functools
import jax
import jax.numpy as jnp
from jax import lax
from jax.experimental import pallas as pl
from jax.experimental.pallas import tpu as pltpu
from jax.sharding import PartitionSpec as P

CH = 64
X = 32
Y = 16
NB = 8
F32 = jnp.float32
BF = jnp.bfloat16
MESH = pl.DeviceIdType.MESH


def lanes(shape):
    return lax.broadcasted_iota(jnp.int32, shape, len(shape) - 1)


def sublanes(shape):
    return lax.broadcasted_iota(jnp.int32, shape, len(shape) - 2)


def build_weights(w, bw):
    zero = jnp.zeros((64, 64), BF)
    wide = jnp.zeros((64, 128), BF)

    def one(k, carry):
        wm, w0, wp = w[3 * k], w[3 * k + 1], w[3 * k + 2]
        a = jnp.concatenate([w0, wm], axis=1)
        b = jnp.concatenate([wp, w0], axis=1)
        c = jnp.concatenate([zero, wp], axis=1)
        d = jnp.concatenate([wm, zero], axis=1)
        for r, (left, right) in enumerate(
            ((a, wide), (b, d), (c, a), (wide, b), (wide, c), (d, wide))
        ):
            bw[k, r * 64 : (r + 1) * 64, 0:128] = left
            bw[k, r * 64 : (r + 1) * 64, 128:256] = right
        return carry

    lax.fori_loop(0, 9, one, 0)


def tile_bias(b, bt):
    for i in range(4):
        bt[:, i * 64 : (i + 1) * 64] = b[...]


def take(v, idx):
    return jnp.concatenate(
        [
            jnp.take_along_axis(v[:, k : k + 128], idx, axis=0, mode="promise_in_bounds")
            for k in range(0, v.shape[1], 128)
        ],
        axis=1,
    )


def pack6(v, zm, zp, low):
    first = jnp.concatenate([v[:, 0:256], jnp.where(low, v[:, 256:384], zm)], axis=1)
    second = jnp.concatenate([v[:, 256:512], jnp.where(low, zp, v[:, 128:256])], axis=1)
    return jnp.concatenate([first, second], axis=0).astype(BF)


def load_cell(s, *at):
    v = s[at].astype(F32)
    return jnp.concatenate([v[0:8], v[8:16]], axis=1)


def body(
    nr,
    nc,
    cin,
    cw,
    cb,
    fin,
    w1,
    b1,
    w2,
    b2,
    ptile,
    pcell,
    nb,
    cout_hbm,
    fout_hbm,
    vin,
    vf,
    vw,
    bw,
    bt,
    edge,
    hx,
    hy,
    hc,
    hf,
    cp,
    cs,
    cout,
    req,
    reqr,
    sel,
    psend,
    precv,
    s1,
    s2,
    fr,
    pad,
    fout,
    lsem,
    hsend,
    hrecv,
    qsend,
    qrecv,
    asend,
    arecv,
    fsend,
    frecv,
):
    r = lax.axis_index("row")
    c = lax.axis_index("col")
    rp, rm = lax.rem(r + 1, nr), lax.rem(r + nr - 1, nr)
    cpl, cmi = lax.rem(c + 1, nc), lax.rem(c + nc - 1, nc)
    me = r * nc + c

    barrier = pltpu.get_barrier_semaphore()
    greet = [(r, lax.rem(c + k, nc)) for k in range(1, nc)]
    greet += [(rp, c), (rm, c), (rp, cpl), (rp, cmi), (rm, cpl), (rm, cmi)]
    for peer in greet:
        pl.semaphore_signal(barrier, inc=1, device_id=peer, device_id_type=MESH)

    loads = [
        pltpu.make_async_copy(cin, vin, lsem.at[0]),
        pltpu.make_async_copy(cw, vw.at[0], lsem.at[1]),
        pltpu.make_async_copy(fin, vf, lsem.at[2]),
        pltpu.make_async_copy(w1, vw.at[1], lsem.at[3]),
        pltpu.make_async_copy(w2, vw.at[2], lsem.at[4]),
    ]
    for copy in loads:
        copy.start()

    tiles = [ptile[b] for b in range(NB)]
    cells = [pcell[b] for b in range(NB)]
    slots = []
    for b in range(NB):
        n = jnp.int32(0)
        for e in range(b):
            n = n + jnp.where(tiles[e] == tiles[b], 1, 0)
        slots.append(n)
    row_id = sublanes((nc * 8, 128))
    wanted = jnp.full((nc * 8, 128), -1, jnp.int32)
    for b in range(NB):
        wanted = jnp.where(row_id == tiles[b] * 8 + slots[b], cells[b], wanted)
    req[...] = wanted.reshape(nc, 8, 128)

    loads[0].wait()
    ei = sublanes((64, 512))
    ej = lanes((64, 512))
    pick = jnp.where(ej == jnp.where(ei < 32, ei * 16 + 15, (ei - 32) * 16), 1.0, 0.0).astype(BF)
    edge[...] = jnp.dot(pick, vin[...].reshape(512, 512), preferred_element_type=F32).astype(BF)

    pl.semaphore_wait(barrier, len(greet))

    halos = []
    for i, (src, dst, peer) in enumerate(
        (
            (edge.at[0:32], hy.at[0], (r, cpl)),
            (edge.at[32:64], hy.at[1], (r, cmi)),
            (vin.at[31], hx.at[0], (rp, c)),
            (vin.at[0], hx.at[1], (rm, c)),
            (edge.at[16:32], hc.at[0], (rp, cpl)),
            (edge.at[48:64], hc.at[1], (rp, cmi)),
            (edge.at[0:16], hc.at[2], (rm, cpl)),
            (edge.at[32:48], hc.at[3], (rm, cmi)),
        )
    ):
        copy = pltpu.make_async_remote_copy(
            src_ref=src,
            dst_ref=dst,
            send_sem=hsend.at[i],
            recv_sem=hrecv.at[i],
            device_id=peer,
            device_id_type=MESH,
        )
        copy.start()
        halos.append(copy)
    asks = []
    for k in range(1, nc):
        d = lax.rem(c + k, nc)
        copy = pltpu.make_async_remote_copy(
            src_ref=req.at[d],
            dst_ref=reqr.at[c],
            send_sem=qsend.at[k],
            recv_sem=qrecv.at[k],
            device_id=(r, d),
            device_id_type=MESH,
        )
        copy.start()
        asks.append(copy)
    reqr[c] = req[c]

    loads[1].wait()
    build_weights(vw.at[0], bw.at[0])
    tile_bias(cb, bt.at[0])
    tile_bias(b1, bt.at[1])
    tile_bias(b2, bt.at[2])

    for copy in halos:
        copy.wait()

    low16 = lanes((16, 128)) < 64
    zero16 = jnp.zeros((16, 128), F32)
    y16 = sublanes((16, 512))
    hf[...] = hy[...].astype(F32)

    def place(at, a, left, right):
        for dy, v in enumerate(
            (
                jnp.where(y16 == 0, left, pltpu.roll(a, 1, 0)),
                a,
                jnp.where(y16 == 15, right, pltpu.roll(a, 15, 0)),
            )
        ):
            o = dy * 384
            cp[at, 0, :, o : o + 256] = v[:, 0:256].astype(BF)
            cp[at, 0, :, o + 256 : o + 384] = jnp.where(low16, v[:, 256:384], zero16).astype(BF)
            cp[at, 1, :, o : o + 256] = v[:, 256:512].astype(BF)
            cp[at, 1, :, o + 256 : o + 384] = jnp.where(low16, zero16, v[:, 128:256]).astype(BF)

    def coarse_one(x, carry):
        left = jnp.where(c > 0, hf[0, pl.ds(x, 1), :], 0.0)
        right = jnp.where(c < nc - 1, hf[1, pl.ds(x, 1), :], 0.0)
        place(x + 1, vin[x].astype(F32), left, right)
        return carry

    lax.fori_loop(0, X, coarse_one, 0)
    for at, ok, i, row, j in ((0, r > 0, 0, 15, 0), (33, r < nr - 1, 1, 0, 2)):
        corner_l = hc[j].astype(F32)[row : row + 1]
        corner_r = hc[j + 1].astype(F32)[row : row + 1]
        place(
            at,
            jnp.where(ok, hx[i].astype(F32), 0.0),
            jnp.where(ok & (c > 0), corner_l, 0.0),
            jnp.where(ok & (c < nc - 1), corner_r, 0.0),
        )

    cbias = bt[0]

    def coarse_conv(i, carry):
        x0 = i * 8
        left = jnp.concatenate(
            [cp[pl.ds(x0 + dx, 8)].reshape(256, 1152) for dx in range(3)], axis=1
        )
        out = jnp.dot(left, bw[0].reshape(3456, 256), preferred_element_type=F32)
        out = jnp.maximum(out + cbias, 0.0).astype(BF).reshape(8, 2, 16, 256)
        cs[pl.ds(x0, 8)] = out
        cout[pl.ds(x0, 8), :, 0:256] = out[:, 0]
        cout[pl.ds(x0, 8), :, 256:512] = out[:, 1]
        return carry

    lax.fori_loop(0, 4, coarse_conv, 0)
    cstore = pltpu.make_async_copy(cout, cout_hbm, lsem.at[5])
    cstore.start()

    for copy in asks:
        copy.wait()
    i16 = sublanes((16, 128))
    l16 = lanes((16, 128))

    def choose(d, carry):
        for s in range(2):
            cell = jnp.broadcast_to(reqr[d, s : s + 1, :], (16, 128))
            px = (cell >> 3) * 4 + (i16 >> 2)
            py = ((cell >> 1) & 3) * 4 + (i16 & 3)
            target = jnp.where(cell >= 0, (px * 2 + (cell & 1)) * 16 + py, -1)
            for k in range(8):
                sel[d, s * 16 : (s + 1) * 16, k * 128 : (k + 1) * 128] = jnp.where(
                    target == l16 + k * 128, 1.0, 0.0
                ).astype(BF)
        return carry

    lax.fori_loop(0, nc, choose, 0)
    psend[...] = (
        jnp.dot(
            sel[...].reshape(nc * 32, 1024),
            cs[...].reshape(1024, 256),
            preferred_element_type=F32,
        )
        .astype(BF)
        .reshape(nc, 32, 256)
    )
    gives = []
    for k in range(1, nc):
        d = lax.rem(c + k, nc)
        copy = pltpu.make_async_remote_copy(
            src_ref=psend.at[d],
            dst_ref=precv.at[c],
            send_sem=asend.at[k],
            recv_sem=arecv.at[k],
            device_id=(r, d),
            device_id_type=MESH,
        )
        copy.start()
        gives.append(copy)
    precv[c] = psend[c]

    loads[3].wait()
    build_weights(vw.at[1], bw.at[1])
    loads[4].wait()
    build_weights(vw.at[2], bw.at[2])
    loads[2].wait()

    b8 = sublanes((8, 128))
    low = lanes((8, 128)) < 64
    index, local, cross = [], [], []
    for f in range(6):
        linked = jnp.full((8, 128), -1, jnp.int32)
        for b in range(NB):
            linked = jnp.where(b8 == b, nb[b, f], linked)
        owner = linked >> 3
        index.append(linked & 7)
        local.append(owner == me)
        other = me + (-nc, nc, -1, 1, -1, 1)[f]
        cross.append((linked >= 0) & (owner == other))

    base = jnp.zeros((8, 128), jnp.int32)
    for b in range(NB):
        base = jnp.where(b8 == b, tiles[b] * 32 + slots[b] * 16, base)
    l8 = lanes((8, 128))
    rows = []
    for q in range(16):
        rows.append(
            jnp.concatenate(
                [
                    jnp.where(base + q == l8 + k * 128, 1.0, 0.0)
                    for k in range(nc * 32 // 128)
                ],
                axis=1,
            )
        )
    sel2 = jnp.concatenate(rows, axis=0).astype(BF)

    for copy in gives:
        copy.wait()
    up = jnp.dot(sel2, precv[...].reshape(nc * 32, 256), preferred_element_type=F32)

    for q in range(16):
        u = up[q * 8 : (q + 1) * 8]
        parts = []
        for k in (0, 128):
            v = u[:, k : k + 128]
            w = pltpu.roll(v, 64, 1)
            parts += [jnp.where(low, v, w), jnp.where(low, w, v)]
        u = jnp.concatenate(parts, axis=1)
        for i in range(2):
            for j in range(2):
                x, y = (q // 4) * 2 + i, (q % 4) * 2 + j
                o = (x * 8 + y) * 512
                v = vf[:, o : o + 512].astype(F32) + u
                s1[x, y] = jnp.concatenate([v[:, 0:256], v[:, 256:512]], axis=0).astype(BF)

    zero8 = jnp.zeros((8, 128), F32)
    corner = jnp.zeros((16, 384), BF)
    for i in (0, 9):
        for j in (0, 9):
            pad[i, j] = corner

    def fine(s, turn, store):
        moves = []
        for i, (src, peer) in enumerate(
            ((s.at[7], (rp, c)), (s.at[0], (rm, c)), (s.at[:, 7], (r, cpl)), (s.at[:, 0], (r, cmi)))
        ):
            copy = pltpu.make_async_remote_copy(
                src_ref=src,
                dst_ref=fr.at[turn, i],
                send_sem=fsend.at[turn, i],
                recv_sem=frecv.at[turn, i],
                device_id=peer,
                device_id_type=MESH,
            )
            copy.start()
            moves.append(copy)

        def inner(x, carry):
            for y in range(8):
                v = load_cell(s, x, y)
                zm = jnp.where(local[4], take(v[:, 384:512], index[4]), 0.0)
                zp = jnp.where(local[5], take(v[:, 0:128], index[5]), 0.0)
                pad[x + 1, y + 1] = pack6(v, zm, zp, low)
            return carry

        lax.fori_loop(0, 8, inner, 0)
        for copy in moves:
            copy.wait()

        def outer(k, carry):
            for f in range(4):
                layer = 7 if f % 2 == 0 else 0
                near = load_cell(s, layer, k) if f < 2 else load_cell(s, k, layer)
                far = load_cell(fr, turn, f, k)
                in_l = jnp.concatenate([local[f]] * 4, axis=1)
                in_c = jnp.concatenate([cross[f]] * 4, axis=1)
                v = jnp.where(
                    in_l, take(near, index[f]), jnp.where(in_c, take(far, index[f]), 0.0)
                )
                edge_at = 0 if f % 2 == 0 else 9
                v = pack6(v, zero8, zero8, low)
                if f < 2:
                    pad[edge_at, k + 1] = v
                else:
                    pad[k + 1, edge_at] = v
            return carry

        lax.fori_loop(0, 8, outer, 0)
        bias = bt[turn + 1]

        def conv(i, carry):
            x0 = i * 2
            left = jnp.concatenate(
                [
                    pad[pl.ds(x0 + dx, 2), dy : dy + 8].reshape(256, 384)
                    for dx in range(3)
                    for dy in range(3)
                ],
                axis=1,
            )
            out = jnp.dot(left, bw[turn + 1].reshape(3456, 256), preferred_element_type=F32)
            store(x0, jnp.maximum(out + bias, 0.0).astype(BF))
            return carry

        lax.fori_loop(0, 4, conv, 0)

    def keep(x0, out):
        s2[pl.ds(x0, 2)] = out.reshape(2, 8, 16, 256)

    def final(x0, out):
        wide = out.astype(F32)
        for i in range(32):
            at = pl.multiple_of(x0 * 4096 + i * 256, 256)
            fout[:, pl.ds(at, 256)] = wide[i * 8 : (i + 1) * 8].astype(BF)

    fine(s1, 0, keep)
    fine(s2, 1, final)
    fstore = pltpu.make_async_copy(fout, fout_hbm, lsem.at[6])
    fstore.start()
    cstore.wait()
    fstore.wait()


def shards(
    coarse_in,
    coarse_weight,
    coarse_bias,
    fine_in,
    weight_first,
    bias_first,
    weight_second,
    bias_second,
    parent_tile,
    parent_cell,
    neighbours,
):
    nr = lax.axis_size("row")
    nc = lax.axis_size("col")
    anywhere = pl.BlockSpec(memory_space=pl.ANY)
    vector = pl.BlockSpec(memory_space=pltpu.VMEM)
    scalar = pl.BlockSpec(memory_space=pltpu.SMEM)
    dma = pltpu.SemaphoreType.DMA
    return pl.pallas_call(
        functools.partial(body, nr, nc),
        out_shape=(
            jax.ShapeDtypeStruct(coarse_in.shape, BF),
            jax.ShapeDtypeStruct(fine_in.shape, BF),
        ),
        in_specs=[
            anywhere,
            anywhere,
            vector,
            anywhere,
            anywhere,
            vector,
            anywhere,
            vector,
            scalar,
            scalar,
            scalar,
        ],
        out_specs=(anywhere, anywhere),
        scratch_shapes=[
            pltpu.VMEM((X, Y, 512), BF),
            pltpu.VMEM((NB, 32768), BF),
            pltpu.VMEM((3, 27, CH, CH), BF),
            pltpu.VMEM((3, 9, 384, 256), BF),
            pltpu.VMEM((3, 1, 256), F32),
            pltpu.VMEM((64, 512), BF),
            pltpu.VMEM((2, 16, 512), BF),
            pltpu.VMEM((2, 32, 512), BF),
            pltpu.VMEM((4, 16, 512), BF),
            pltpu.VMEM((2, 32, 512), F32),
            pltpu.VMEM((34, 2, 16, 1152), BF),
            pltpu.VMEM((X, 2, 16, 256), BF),
            pltpu.VMEM((X, Y, 512), BF),
            pltpu.VMEM((nc, 8, 128), jnp.int32),
            pltpu.VMEM((nc, 8, 128), jnp.int32),
            pltpu.VMEM((nc, 32, 1024), BF),
            pltpu.VMEM((nc, 32, 256), BF),
            pltpu.VMEM((nc, 32, 256), BF),
            pltpu.VMEM((8, 8, 16, 256), BF),
            pltpu.VMEM((8, 8, 16, 256), BF),
            pltpu.VMEM((2, 4, 8, 16, 256), BF),
            pltpu.VMEM((10, 10, 16, 384), BF),
            pltpu.VMEM((NB, 32768), BF),
            dma((7,)),
            dma((8,)),
            dma((8,)),
            dma((nc,)),
            dma((nc,)),
            dma((nc,)),
            dma((nc,)),
            dma((2, 4)),
            dma((2, 4)),
        ],
        compiler_params=pltpu.CompilerParams(collective_id=0, has_side_effects=True),
    )(
        coarse_in,
        coarse_weight,
        coarse_bias.reshape(1, CH),
        fine_in,
        weight_first,
        bias_first.reshape(1, CH),
        weight_second,
        bias_second.reshape(1, CH),
        parent_tile.reshape(NB),
        parent_cell,
        neighbours,
    )


def solution(mesh):
    placed = (
        P("row", "col", None),
        P(),
        P(),
        P(("row", "col"), None),
        P(),
        P(),
        P(),
        P(),
        P(("row", "col"), None),
        P(("row", "col")),
        P(("row", "col"), None),
    )
    return jax.shard_map(
        shards,
        mesh=mesh,
        in_specs=placed,
        out_specs=(P("row", "col", None), P(("row", "col"), None)),
        check_vma=False,
    )
```

profile of v0, /device:TPU:4, one launch (start us, length us, event | category | flops | bytes accessed | tf_op | source)
XLA Modules:
  0.0 44.4 jit_solution(7917902808328358396)
XLA Ops:
  0.6 41.1 %shard_map.122 = (bf16[32,16,512]{2,1,0:T(8,128)(2,1)}, bf16[8,32768]{1,0:T(8,128)(2,1)}) custom-call(bf16[32,16,512]{2,1,0:T(8,128)(2,1)} %cin.1, bf16[27,64,64]{2,1,0:T(8,128)(2,1)} %cw.1, f32[1,64]{1,0:T(1,128)} %bitcast.4, bf16[8,32768]{1,0:T(8,128)(2,1)} %fin.1, bf16[27,64,64]{2,1,0:T(8,128)(2,1)} %w1.1, f32[1,64]{1,0:T(1,128)} %bitcast.5, ...), custom_call_target="tpu_custom_call" | custom-call | tf_op jit(solution)/shard_map/pallas_call | solution.py:470
  41.7 0.0 copy-start
  41.7 1.9 %copy.15 = bf16[32,16,512]{2,1,0:T(8,128)(2,1)} copy(bf16[32,16,512]{2,1,0:T(8,128)(2,1)} %get-tuple-element.4) | data formatting | bytes 1048576
  43.6 0.0 copy-done
  43.6 0.8 %copy.16 = bf16[8,32768]{1,0:T(8,128)(2,1)} copy(bf16[8,32768]{1,0:T(8,128)(2,1)S(1)} %copy-done) | data formatting | bytes 1048576
Async XLA Ops:
  41.7 1.9 %copy-start = (bf16[8,32768]{1,0:T(8,128)(2,1)S(1)}, bf16[8,32768]{1,0:T(8,128)(2,1)}, u32[]{:S(2)}) copy-start(bf16[8,32768]{1,0:T(8,128)(2,1)} %get-tuple-element.5) | copy-start | bytes 1572868
where the time goes:
time: 44.6 us; the launch traced here: 44.4 us
  Pallas kernels  41.1 us (92%)
  local copies, waits for them, and re-layouts  2.72 us (6%)
  between operations  0.65 us (1%)
    pallas_call x1, Pallas kernels, shards(): pl.pallas_call(functools.partial(body, nr, nc), out_shape=(jax.ShapeDtype...  41.1 us
    unnamed x4, local copies, waits for them, and re-layouts  2.72 us

commit v1 on v0

v1 whole, which is shorter than its diff:
```python
import functools
import jax
import jax.numpy as jnp
from jax import lax
from jax.experimental import pallas as pl
from jax.experimental.pallas import tpu as pltpu
from jax.sharding import PartitionSpec as P

CH = 64
X = 32
Y = 16
NB = 8
F32 = jnp.float32
BF = jnp.bfloat16
MESH = pl.DeviceIdType.MESH


def lanes(shape):
    return lax.broadcasted_iota(jnp.int32, shape, len(shape) - 1)


def sublanes(shape):
    return lax.broadcasted_iota(jnp.int32, shape, len(shape) - 2)


def build_weights(w, bw):
    zero = jnp.zeros((64, 64), BF)
    wide = jnp.zeros((64, 128), BF)

    def one(k, carry):
        wm, w0, wp = w[3 * k], w[3 * k + 1], w[3 * k + 2]
        a = jnp.concatenate([w0, wm], axis=1)
        b = jnp.concatenate([wp, w0], axis=1)
        c = jnp.concatenate([zero, wp], axis=1)
        d = jnp.concatenate([wm, zero], axis=1)
        for r, (left, right) in enumerate(
            ((a, wide), (b, d), (c, a), (wide, b), (wide, c), (d, wide))
        ):
            bw[k, r * 64 : (r + 1) * 64, 0:128] = left
            bw[k, r * 64 : (r + 1) * 64, 128:256] = right
        return carry

    lax.fori_loop(0, 9, one, 0)


def tile_bias(b, bt):
    for i in range(4):
        bt[:, i * 64 : (i + 1) * 64] = b[...]


def take(v, idx):
    return jnp.concatenate(
        [
            jnp.take_along_axis(v[:, k : k + 128], idx, axis=0, mode="promise_in_bounds")
            for k in range(0, v.shape[1], 128)
        ],
        axis=1,
    )


def pack6(v, zm, zp, low):
    first = jnp.concatenate([v[:, 0:256], jnp.where(low, v[:, 256:384], zm)], axis=1)
    second = jnp.concatenate([v[:, 256:512], jnp.where(low, zp, v[:, 128:256])], axis=1)
    return jnp.concatenate([first, second], axis=0).astype(BF)


def load_cell(s, *at):
    v = s[at].astype(F32)
    return jnp.concatenate([v[0:8], v[8:16]], axis=1)


def order(nc):
    side = {16: 4, 4: 2}[nc]
    dist = lambda v: min(v, side - v)
    pairs = [(a, b) for a in range(side) for b in range(side)]
    return side, sorted(pairs, key=lambda p: -dist(p[0]) - dist(p[1]))


def body(
    nr,
    nc,
    cin,
    cw,
    cb,
    fin,
    w1,
    b1,
    w2,
    b2,
    ptile,
    pcell,
    nb,
    cout,
    fout,
    vin,
    vf,
    vw,
    bw,
    bt,
    edge,
    hx,
    hy,
    hc,
    yl,
    cp,
    cacc,
    cs,
    req,
    reqr,
    sel,
    psend,
    precv,
    s1,
    s2,
    fr,
    pad,
    facc,
    lsem,
    hsend,
    hrecv,
    qsend,
    qrecv,
    asend,
    arecv,
    fsend,
    frecv,
):
    r = lax.axis_index("row")
    c = lax.axis_index("col")
    rp, rm = lax.rem(r + 1, nr), lax.rem(r + nr - 1, nr)
    cpl, cmi = lax.rem(c + 1, nc), lax.rem(c + nc - 1, nc)
    me = r * nc + c
    side, offsets = order(nc)
    cy, cz = lax.div(c, side), lax.rem(c, side)
    peers = [lax.rem(cy + a, side) * side + lax.rem(cz + b, side) for a, b in offsets]
    barrier = pltpu.get_barrier_semaphore()
    greet = [(r, d) for d in peers[:-1]]
    greet += [(rp, c), (rm, c), (rp, cpl), (rp, cmi), (rm, cpl), (rm, cmi)]
    for peer in greet:
        pl.semaphore_signal(barrier, inc=1, device_id=peer, device_id_type=MESH)

    loads = [
        pltpu.make_async_copy(cin, vin, lsem.at[0]),
        pltpu.make_async_copy(cw, vw.at[0], lsem.at[1]),
        pltpu.make_async_copy(fin, vf, lsem.at[2]),
        pltpu.make_async_copy(w1, vw.at[1], lsem.at[3]),
        pltpu.make_async_copy(w2, vw.at[2], lsem.at[4]),
    ]
    for copy in loads:
        copy.start()
    sends = []

    def send(src, dst, ssem, rsem, peer):
        copy = pltpu.make_async_remote_copy(
            src_ref=src,
            dst_ref=dst,
            send_sem=ssem,
            recv_sem=rsem,
            device_id=peer,
            device_id_type=MESH,
        )
        copy.start()
        sends.append(copy)
        return copy

    tiles = [ptile[b] for b in range(NB)]
    cells = [pcell[b] for b in range(NB)]
    slots = []
    for b in range(NB):
        n = jnp.int32(0)
        for e in range(b):
            n = n + jnp.where(tiles[e] == tiles[b], 1, 0)
        slots.append(n)
    row_id = sublanes((nc * 8, 128))
    wanted = jnp.full((nc * 8, 128), -1, jnp.int32)
    for b in range(NB):
        wanted = jnp.where(row_id == tiles[b] * 8 + slots[b], cells[b], wanted)
    req[...] = wanted.reshape(nc, 8, 128)

    loads[0].wait()
    ei = sublanes((64, 512))
    ej = lanes((64, 512))
    pick = jnp.where(ej == jnp.where(ei < 32, ei * 16 + 15, (ei - 32) * 16), 1.0, 0.0).astype(BF)
    edge[...] = jnp.dot(pick, vin[...].reshape(512, 512), preferred_element_type=F32).astype(BF)
    loads[1].wait()
    build_weights(vw.at[0], bw.at[0])
    tile_bias(cb, bt.at[0])
    tile_bias(b1, bt.at[1])
    tile_bias(b2, bt.at[2])
    pl.semaphore_wait(barrier, len(greet))
    halos = [
        send(src, dst, hsend.at[i], hrecv.at[i], peer)
        for i, (src, dst, peer) in enumerate(
            (
                (edge.at[16:32], hc.at[0], (rp, cpl)),
                (edge.at[48:64], hc.at[1], (rp, cmi)),
                (edge.at[0:16], hc.at[2], (rm, cpl)),
                (edge.at[32:48], hc.at[3], (rm, cmi)),
                (edge.at[0:32], hy.at[0], (r, cpl)),
                (edge.at[32:64], hy.at[1], (r, cmi)),
                (vin.at[31], hx.at[0], (rp, c)),
                (vin.at[0], hx.at[1], (rm, c)),
            )
        )
    ]
    asks = [
        send(req.at[d], reqr.at[c], qsend.at[k], qrecv.at[k], (r, d))
        for k, d in enumerate(peers[:-1])
    ]
    reqr[c] = req[c]

    low16 = lanes((16, 128)) < 64
    zero16 = jnp.zeros((16, 128), F32)
    y16 = sublanes((16, 512))

    def place(at, a, left, right):
        for dy, v in enumerate(
            (
                jnp.where(y16 == 0, left, pltpu.roll(a, 1, 0)),
                a,
                jnp.where(y16 == 15, right, pltpu.roll(a, 15, 0)),
            )
        ):
            o = dy * 384
            cp[at, 0, :, o : o + 256] = v[:, 0:256].astype(BF)
            cp[at, 0, :, o + 256 : o + 384] = jnp.where(low16, v[:, 256:384], zero16).astype(BF)
            cp[at, 1, :, o : o + 256] = v[:, 256:512].astype(BF)
            cp[at, 1, :, o + 256 : o + 384] = jnp.where(low16, zero16, v[:, 128:256]).astype(BF)

    def coarse_one(x, carry):
        place(x + 1, vin[x].astype(F32), 0.0, 0.0)
        return carry

    lax.fori_loop(0, X, coarse_one, 0)
    blank = jnp.zeros((2, 16, 1152), BF)
    cp[0] = blank
    cp[33] = blank
    cbias = bt[0]

    def coarse_conv(i, carry):
        x0 = i * 16
        left = jnp.concatenate(
            [cp[pl.ds(x0 + dx, 16)].reshape(512, 1152) for dx in range(3)], axis=1
        )
        out = jnp.dot(left, bw[0].reshape(3456, 256), preferred_element_type=F32)
        cacc[pl.ds(x0, 16)] = (out + cbias).reshape(16, 2, 16, 256)
        return carry

    lax.fori_loop(0, 2, coarse_conv, 0)

    for copy in asks:
        copy.wait_recv()
    i16 = sublanes((16, 128))
    l16 = lanes((16, 128))
    for k, d in enumerate(peers):
        for s in range(2):
            cell = jnp.broadcast_to(reqr[d, s : s + 1, :], (16, 128))
            px = (cell >> 3) * 4 + (i16 >> 2)
            py = ((cell >> 1) & 3) * 4 + (i16 & 3)
            target = jnp.where(cell >= 0, (px * 2 + (cell & 1)) * 16 + py, -1)
            for j in range(8):
                sel[k, s * 16 : (s + 1) * 16, j * 128 : (j + 1) * 128] = jnp.where(
                    target == l16 + j * 128, 1.0, 0.0
                ).astype(BF)
    for copy in halos:
        copy.wait_recv()

    for at, ok, i, row, j in ((0, r > 0, 0, 15, 0), (33, r < nr - 1, 1, 0, 2)):
        corner_l = hc[j].astype(F32)[row : row + 1]
        corner_r = hc[j + 1].astype(F32)[row : row + 1]
        place(
            at,
            jnp.where(ok, hx[i].astype(F32), 0.0),
            jnp.where(ok & (c > 0), corner_l, 0.0),
            jnp.where(ok & (c < nc - 1), corner_r, 0.0),
        )
    low32 = lanes((32, 128)) < 64
    x32 = sublanes((32, 256))
    for i, ok in enumerate((c > 0, c < nc - 1)):
        v = jnp.where(ok, hy[i].astype(F32), 0.0)
        left = jnp.concatenate(
            [
                jnp.concatenate([v[:, 0:256], jnp.where(low32, v[:, 256:384], 0.0)], axis=1),
                jnp.concatenate([v[:, 256:512], jnp.where(low32, 0.0, v[:, 128:256])], axis=1),
            ],
            axis=0,
        ).astype(BF)
        part = [
            jnp.dot(left, bw[0, 3 * dx + 2 * i], preferred_element_type=F32) for dx in range(3)
        ]
        for g in range(2):
            before, here, after = [p[g * 32 : (g + 1) * 32] for p in part]
            yl[i, g] = (
                here
                + jnp.where(x32 == 0, 0.0, pltpu.roll(before, 1, 0))
                + jnp.where(x32 == 31, 0.0, pltpu.roll(after, 31, 0))
            )
    for at, x, k in ((0, 0, 0), (33, 31, 6)):
        cacc[x] = cacc[x] + jnp.dot(
            cp[at].reshape(32, 1152),
            bw[0, k : k + 3].reshape(1152, 256),
            preferred_element_type=F32,
        ).reshape(2, 16, 256)
    y256 = sublanes((16, 256))

    def coarse_out(x, carry):
        for g in range(2):
            v = cacc[x, g]
            v = v + jnp.where(y256 == 0, yl[0, g, pl.ds(x, 1), :], 0.0)
            v = v + jnp.where(y256 == 15, yl[1, g, pl.ds(x, 1), :], 0.0)
            v = jnp.maximum(v, 0.0).astype(BF)
            cs[x, g] = v
            cout[x, :, g * 256 : (g + 1) * 256] = v
        return carry

    lax.fori_loop(0, X, coarse_out, 0, unroll=2)
    gives = []
    for m in range(0, nc, 4):
        psend[m : m + 4] = (
            jnp.dot(
                sel[m : m + 4].reshape(128, 1024),
                cs[...].reshape(1024, 256),
                preferred_element_type=F32,
            )
            .astype(BF)
            .reshape(4, 32, 256)
        )
        for k in range(m, m + 4):
            if k < nc - 1:
                gives.append(
                    send(psend.at[k], precv.at[c], asend.at[k], arecv.at[k], (r, peers[k]))
                )
    precv[c] = psend[nc - 1]
    loads[3].wait()
    build_weights(vw.at[1], bw.at[1])
    loads[4].wait()
    build_weights(vw.at[2], bw.at[2])
    loads[2].wait()
    b8 = sublanes((8, 128))
    low = lanes((8, 128)) < 64
    index, local, cross = [], [], []
    for f in range(6):
        linked = jnp.full((8, 128), -1, jnp.int32)
        for b in range(NB):
            linked = jnp.where(b8 == b, nb[b, f], linked)
        owner = linked >> 3
        index.append(linked & 7)
        local.append(owner == me)
        other = me + (-nc, nc, -1, 1, -1, 1)[f]
        cross.append((linked >= 0) & (owner == other))

    base = jnp.zeros((8, 128), jnp.int32)
    for b in range(NB):
        base = jnp.where(b8 == b, tiles[b] * 32 + slots[b] * 16, base)
    l8 = lanes((8, 128))
    rows = []
    for q in range(16):
        rows.append(
            jnp.concatenate(
                [
                    jnp.where(base + q == l8 + k * 128, 1.0, 0.0)
                    for k in range(nc * 32 // 128)
                ],
                axis=1,
            )
        )
    sel2 = jnp.concatenate(rows, axis=0).astype(BF)

    zero8 = jnp.zeros((8, 128), F32)
    blank = jnp.zeros((16, 384), BF)
    for turn in range(2):
        for i in range(10):
            for j in range(10):
                if i in (0, 9) or j in (0, 9):
                    pad[turn, i, j] = blank
    for copy in gives:
        copy.wait_recv()
    up = jnp.dot(sel2, precv[...].reshape(nc * 32, 256), preferred_element_type=F32)
    grown = []
    for q in range(16):
        u = up[q * 8 : (q + 1) * 8]
        parts = []
        for k in (0, 128):
            v = u[:, k : k + 128]
            w = pltpu.roll(v, 64, 1)
            parts += [jnp.where(low, v, w), jnp.where(low, w, v)]
        grown.append(jnp.concatenate(parts, axis=1))

    def begin(x, y):
        o = (x * 8 + y) * 512
        v = vf[:, o : o + 512].astype(F32) + grown[(x // 2) * 4 + y // 2]
        s1[x, y] = jnp.concatenate([v[:, 0:256], v[:, 256:512]], axis=0).astype(BF)

    def send_y(s, turn):
        return [
            send(s.at[:, 7], fr.at[turn, 2], fsend.at[turn, 2], frecv.at[turn, 2], (r, cpl)),
            send(s.at[:, 0], fr.at[turn, 3], fsend.at[turn, 3], frecv.at[turn, 3], (r, cmi)),
        ]

    def send_x(s, turn):
        return [
            send(s.at[7], fr.at[turn, 0], fsend.at[turn, 0], frecv.at[turn, 0], (rp, c)),
            send(s.at[0], fr.at[turn, 1], fsend.at[turn, 1], frecv.at[turn, 1], (rm, c)),
        ]

    inside = range(1, 7)
    for x in range(8):
        begin(x, 0)
        begin(x, 7)
    ymoves = send_y(s1, 0)
    for y in inside:
        begin(0, y)
        begin(7, y)
    moves = send_x(s1, 0) + ymoves
    for x in inside:
        for y in inside:
            begin(x, y)

    def fine_main(s, turn):
        def inner(x, carry):
            for y in range(8):
                v = load_cell(s, x, y)
                zm = jnp.where(local[4], take(v[:, 384:512], index[4]), 0.0)
                zp = jnp.where(local[5], take(v[:, 0:128], index[5]), 0.0)
                pad[turn, x + 1, y + 1] = pack6(v, zm, zp, low)
            return carry

        lax.fori_loop(0, 8, inner, 0)
        bias = bt[turn + 1]

        def conv(i, carry):
            x0 = i * 4
            left = jnp.concatenate(
                [
                    pad[turn, pl.ds(x0 + dx, 4), dy : dy + 8].reshape(512, 384)
                    for dx in range(3)
                    for dy in range(3)
                ],
                axis=1,
            )
            out = jnp.dot(left, bw[turn + 1].reshape(3456, 256), preferred_element_type=F32)
            facc[pl.ds(x0, 4)] = (out + bias).reshape(4, 8, 16, 256)
            return carry

        lax.fori_loop(0, 2, conv, 0)

    def fine_fix(s, turn, moves):
        for f in range(4):
            moves[f].wait_recv()
            layer, at, tap = (7, 0, 0) if f % 2 == 0 else (0, 9, 2)
            in_l = jnp.concatenate([local[f]] * 4, axis=1)
            in_c = jnp.concatenate([cross[f]] * 4, axis=1)
            for k in range(8):
                near = load_cell(s, layer, k) if f < 2 else load_cell(s, k, layer)
                far = load_cell(fr, turn, f, k)
                v = jnp.where(
                    in_l, take(near, index[f]), jnp.where(in_c, take(far, index[f]), 0.0)
                )
                v = pack6(v, zero8, zero8, low)
                if f < 2:
                    pad[turn, at, k + 1] = v
                else:
                    pad[turn, k + 1, at] = v
            if f < 2:
                left = [pad[turn, at, d : d + 8].reshape(128, 384) for d in range(3)]
                right = bw[turn + 1, 3 * tap : 3 * tap + 3].reshape(1152, 256)
            else:
                left = [pad[turn, d : d + 8, at].reshape(128, 384) for d in range(3)]
                right = jnp.concatenate([bw[turn + 1, 3 * d + tap] for d in range(3)], axis=0)
            add = jnp.dot(
                jnp.concatenate(left, axis=1), right, preferred_element_type=F32
            ).reshape(8, 16, 256)
            if f < 2:
                facc[7 - layer] = facc[7 - layer] + add
            else:
                facc[:, 7 - layer] = facc[:, 7 - layer] + add

    def keep(x, y):
        s2[x, y] = jnp.maximum(facc[x, y], 0.0).astype(BF)

    def final(x, y):
        v = jnp.maximum(facc[x, y], 0.0)
        at = pl.multiple_of((x * 8 + y) * 512, 512)
        fout[:, pl.ds(at, 512)] = jnp.concatenate([v[0:8], v[8:16]], axis=1).astype(BF)

    def each_inside(put):
        def one(x, carry):
            for y in inside:
                put(x, y)
            return carry

        lax.fori_loop(1, 7, one, 0)

    fine_main(s1, 0)
    each_inside(keep)
    fine_fix(s1, 0, moves)
    for x in range(8):
        keep(x, 0)
        keep(x, 7)
    ymoves = send_y(s2, 1)
    for y in inside:
        keep(0, y)
        keep(7, y)
    moves = send_x(s2, 1) + ymoves
    fine_main(s2, 1)
    each_inside(final)
    fine_fix(s2, 1, moves)
    for x in range(8):
        final(x, 0)
        final(x, 7)
    for y in inside:
        final(0, y)
        final(7, y)
    for copy in sends:
        copy.wait_send()


def put_out(coarse, fine, coarse_hbm, fine_hbm, sem):
    copies = [
        pltpu.make_async_copy(coarse, coarse_hbm, sem.at[0]),
        pltpu.make_async_copy(fine, fine_hbm, sem.at[1]),
    ]
    for copy in copies:
        copy.start()
    for copy in copies:
        copy.wait()


def shards(
    coarse_in,
    coarse_weight,
    coarse_bias,
    fine_in,
    weight_first,
    bias_first,
    weight_second,
    bias_second,
    parent_tile,
    parent_cell,
    neighbours,
):
    nr = lax.axis_size("row")
    nc = lax.axis_size("col")
    anywhere = pl.BlockSpec(memory_space=pl.ANY)
    vector = pl.BlockSpec(memory_space=pltpu.VMEM)
    scalar = pl.BlockSpec(memory_space=pltpu.SMEM)
    dma = pltpu.SemaphoreType.DMA
    coarse, fine = pl.pallas_call(
        functools.partial(body, nr, nc),
        out_shape=(pltpu.VMEM(coarse_in.shape, BF), pltpu.VMEM(fine_in.shape, BF)),
        in_specs=[anywhere, anywhere, vector, anywhere, anywhere, vector, anywhere, vector]
        + [scalar] * 3,
        out_specs=(vector, vector),
        scratch_shapes=[
            pltpu.VMEM((X, Y, 512), BF),
            pltpu.VMEM((NB, 32768), BF),
            pltpu.VMEM((3, 27, CH, CH), BF),
            pltpu.VMEM((3, 9, 384, 256), BF),
            pltpu.VMEM((3, 1, 256), F32),
            pltpu.VMEM((64, 512), BF),
            pltpu.VMEM((2, 16, 512), BF),
            pltpu.VMEM((2, 32, 512), BF),
            pltpu.VMEM((4, 16, 512), BF),
            pltpu.VMEM((2, 2, 32, 256), F32),
            pltpu.VMEM((34, 2, 16, 1152), BF),
            pltpu.VMEM((X, 2, 16, 256), F32),
            pltpu.VMEM((X, 2, 16, 256), BF),
            pltpu.VMEM((nc, 8, 128), jnp.int32),
            pltpu.VMEM((nc, 8, 128), jnp.int32),
            pltpu.VMEM((nc, 32, 1024), BF),
            pltpu.VMEM((nc, 32, 256), BF),
            pltpu.VMEM((nc, 32, 256), BF),
            pltpu.VMEM((8, 8, 16, 256), BF),
            pltpu.VMEM((8, 8, 16, 256), BF),
            pltpu.VMEM((2, 4, 8, 16, 256), BF),
            pltpu.VMEM((2, 10, 10, 16, 384), BF),
            pltpu.VMEM((8, 8, 16, 256), F32),
            dma((5,)),
            dma((8,)),
            dma((8,)),
            dma((nc,)),
            dma((nc,)),
            dma((nc,)),
            dma((nc,)),
            dma((2, 4)),
            dma((2, 4)),
        ],
        compiler_params=pltpu.CompilerParams(collective_id=0, has_side_effects=True),
    )(
        coarse_in,
        coarse_weight,
        coarse_bias.reshape(1, CH),
        fine_in,
        weight_first,
        bias_first.reshape(1, CH),
        weight_second,
        bias_second.reshape(1, CH),
        parent_tile.reshape(NB),
        parent_cell,
        neighbours,
    )
    return pl.pallas_call(
        put_out,
        out_shape=(
            jax.ShapeDtypeStruct(coarse_in.shape, BF),
            jax.ShapeDtypeStruct(fine_in.shape, BF),
        ),
        in_specs=[anywhere, anywhere],
        out_specs=(anywhere, anywhere),
        scratch_shapes=[dma((2,))],
        compiler_params=pltpu.CompilerParams(vmem_limit_bytes=1 << 20),
    )(coarse, fine)


def solution(mesh):
    placed = (
        P("row", "col", None),
        P(),
        P(),
        P(("row", "col"), None),
        P(),
        P(),
        P(),
        P(),
        P(("row", "col"), None),
        P(("row", "col")),
        P(("row", "col"), None),
    )
    return jax.shard_map(
        shards,
        mesh=mesh,
        in_specs=placed,
        out_specs=(P("row", "col", None), P(("row", "col"), None)),
        check_vma=False,
    )
```

time: 44.6 us -> 34.7 us (0.78)
  the two profiles are of different devices: /device:TPU:4 before, /device:TPU:1 now
where the time goes in v1:
time: 34.7 us; the launch traced here: 34.1 us
  Pallas kernels  33.5 us (97%)
  between operations  0.64 us (2%)
    pallas_call x1, Pallas kernels, shards(): pl.pallas_call(functools.partial(body, nr, nc), out_shape=(pltpu.VMEM(coa...  32.5 us
    pallas_call x1, Pallas kernels, shards(): pl.pallas_call(put_out, out_shape=(jax.ShapeDtypeStruct(coarse_in.shape,...  0.99 us

profile of v1, /device:TPU:1, one launch (start us, length us, event | category | flops | bytes accessed | tf_op | source)
XLA Modules:
  0.0 34.1 jit_solution(11307605625117990330)
XLA Ops:
  0.6 32.5 %shard_map.122 = (bf16[32,16,512]{2,1,0:T(8,128)(2,1)S(1)}, bf16[8,32768]{1,0:T(8,128)(2,1)S(1)}) custom-call(bf16[32,16,512]{2,1,0:T(8,128)(2,1)} %cin.1, bf16[27,64,64]{2,1,0:T(8,128)(2,1)} %cw.1, f32[1,64]{1,0:T(1,128)} %bitcast.4, bf16[8,32768]{1,0:T(8,128)(2,1)} %fin.1, bf16[27,64,64]{2,1,0:T(8,128)(2,1)} %w1.1, f32[1,64]{1,0:T(1,128)} %bitcast.5, ...), custom_call_target="tpu_custom_call" | custom-call | tf_op jit(solution)/shard_map/pallas_call | solution.py:548
  33.2 1.0 %shard_map.123 = (bf16[32,16,512]{2,1,0:T(8,128)(2,1)}, bf16[8,32768]{1,0:T(8,128)(2,1)}) custom-call(bf16[32,16,512]{2,1,0:T(8,128)(2,1)S(1)} %get-tuple-element.4.coarse, bf16[8,32768]{1,0:T(8,128)(2,1)S(1)} %get-tuple-element.5.fine), custom_call_target="tpu_custom_call" | custom-call | tf_op jit(solution)/shard_map/pallas_call | solution.py:602

commit v2 on v1

--- a/solution.py
+++ b/solution.py
@@ -10,6 +10,7 @@
 X = 32
 Y = 16
 NB = 8
+PARTS = 2
 F32 = jnp.float32
 BF = jnp.bfloat16
 MESH = pl.DeviceIdType.MESH
@@ -87,17 +88,22 @@
     b1,
     w2,
     b2,
+    ptile_in,
+    pcell_in,
+    nb_in,
+    cout,
+    fout,
     ptile,
     pcell,
     nb,
-    cout,
-    fout,
+    braw,
     vin,
     vf,
     vw,
     bw,
     bt,
     edge,
+    crn,
     hx,
     hy,
     hc,
@@ -118,40 +124,57 @@
     lsem,
     hsend,
     hrecv,
-    qsend,
-    qrecv,
-    asend,
-    arecv,
-    fsend,
+    asem,
+    gsem,
     frecv,
 ):
     r = lax.axis_index("row")
     c = lax.axis_index("col")
-    rp, rm = lax.rem(r + 1, nr), lax.rem(r + nr - 1, nr)
-    cpl, cmi = lax.rem(c + 1, nc), lax.rem(c + nc - 1, nc)
     me = r * nc + c
     side, offsets = order(nc)
     cy, cz = lax.div(c, side), lax.rem(c, side)
     peers = [lax.rem(cy + a, side) * side + lax.rem(cz + b, side) for a, b in offsets]
+    up, down, right, left = r < nr - 1, r > 0, c < nc - 1, c > 0
     barrier = pltpu.get_barrier_semaphore()
-    greet = [(r, d) for d in peers[:-1]]
-    greet += [(rp, c), (rm, c), (rp, cpl), (rp, cmi), (rm, cpl), (rm, cmi)]
-    for peer in greet:
-        pl.semaphore_signal(barrier, inc=1, device_id=peer, device_id_type=MESH)
+    near = [
+        ((r, c + 1), right),
+        ((r, c - 1), left),
+        ((r + 1, c), up),
+        ((r - 1, c), down),
+        ((r + 1, c + 1), up & right),
+        ((r + 1, c - 1), up & left),
+        ((r - 1, c + 1), down & right),
+        ((r - 1, c - 1), down & left),
+    ]
+    heard = jnp.int32(nc - 1)
+    for d in peers[:-1]:
+        pl.semaphore_signal(barrier, inc=1, device_id=(r, d), device_id_type=MESH)
+    for peer, there in near[2:]:
+        heard = heard + jnp.where(there, 1, 0)
+
+        @pl.when(there)
+        def _(peer=peer):
+            pl.semaphore_signal(barrier, inc=1, device_id=peer, device_id_type=MESH)
 
     loads = [
         pltpu.make_async_copy(cin, vin, lsem.at[0]),
+        pltpu.make_async_copy(ptile_in, ptile, lsem.at[5]),
+        pltpu.make_async_copy(pcell_in, pcell, lsem.at[6]),
         pltpu.make_async_copy(cw, vw.at[0], lsem.at[1]),
+        pltpu.make_async_copy(nb_in, nb, lsem.at[7]),
+        pltpu.make_async_copy(cb, braw.at[0], lsem.at[8]),
+        pltpu.make_async_copy(b1, braw.at[1], lsem.at[9]),
+        pltpu.make_async_copy(b2, braw.at[2], lsem.at[10]),
         pltpu.make_async_copy(fin, vf, lsem.at[2]),
         pltpu.make_async_copy(w1, vw.at[1], lsem.at[3]),
         pltpu.make_async_copy(w2, vw.at[2], lsem.at[4]),
     ]
+    lin, ltile, lcell, lcw, lnb, lb0, lb1, lb2, lfin, lw1, lw2 = loads
     for copy in loads:
         copy.start()
-    sends = []
-
-    def send(src, dst, ssem, rsem, peer):
-        copy = pltpu.make_async_remote_copy(
+
+    def remote(src, dst, ssem, rsem, peer):
+        return pltpu.make_async_remote_copy(
             src_ref=src,
             dst_ref=dst,
             send_sem=ssem,
@@ -159,10 +182,23 @@
             device_id=peer,
             device_id_type=MESH,
         )
-        copy.start()
-        sends.append(copy)
-        return copy
-
+
+    def start(copy, there):
+        @pl.when(there)
+        def _():
+            copy.start()
+
+    def sent(copy, there):
+        @pl.when(there)
+        def _():
+            copy.wait_send()
+
+    def came(copy, there):
+        @pl.when(there)
+        def _():
+            copy.wait_recv()
+    ltile.wait()
+    lcell.wait()
     tiles = [ptile[b] for b in range(NB)]
     cells = [pcell[b] for b in range(NB)]
     slots = []
@@ -171,42 +207,55 @@
         for e in range(b):
             n = n + jnp.where(tiles[e] == tiles[b], 1, 0)
         slots.append(n)
-    row_id = sublanes((nc * 8, 128))
-    wanted = jnp.full((nc * 8, 128), -1, jnp.int32)
+    row_id = sublanes((nc, 128))
+    wanted = jnp.zeros((nc, 128), jnp.int32)
     for b in range(NB):
-        wanted = jnp.where(row_id == tiles[b] * 8 + slots[b], cells[b], wanted)
-    req[...] = wanted.reshape(nc, 8, 128)
-
-    loads[0].wait()
+        ask = (cells[b] + 1) * jnp.where(slots[b] == 0, 1, 128)
+        wanted = wanted + jnp.where(row_id == tiles[b], ask, 0)
+    for t in range(nc):
+        req[t] = wanted[t : t + 1]
+
+    lin.wait()
     ei = sublanes((64, 512))
     ej = lanes((64, 512))
     pick = jnp.where(ej == jnp.where(ei < 32, ei * 16 + 15, (ei - 32) * 16), 1.0, 0.0).astype(BF)
-    edge[...] = jnp.dot(pick, vin[...].reshape(512, 512), preferred_element_type=F32).astype(BF)
-    loads[1].wait()
+    found = jnp.dot(pick, vin[...].reshape(512, 512), preferred_element_type=F32)
+    edge[...] = found.astype(BF)
+    for i, row in enumerate((31, 63, 0, 32)):
+        crn[i] = found[row : row + 1]
+    lcw.wait()
     build_weights(vw.at[0], bw.at[0])
-    tile_bias(cb, bt.at[0])
-    tile_bias(b1, bt.at[1])
-    tile_bias(b2, bt.at[2])
-    pl.semaphore_wait(barrier, len(greet))
-    halos = [
-        send(src, dst, hsend.at[i], hrecv.at[i], peer)
-        for i, (src, dst, peer) in enumerate(
-            (
-                (edge.at[16:32], hc.at[0], (rp, cpl)),
-                (edge.at[48:64], hc.at[1], (rp, cmi)),
-                (edge.at[0:16], hc.at[2], (rm, cpl)),
-                (edge.at[32:48], hc.at[3], (rm, cmi)),
-                (edge.at[0:32], hy.at[0], (r, cpl)),
-                (edge.at[32:64], hy.at[1], (r, cmi)),
-                (vin.at[31], hx.at[0], (rp, c)),
-                (vin.at[0], hx.at[1], (rm, c)),
-            )
+    lb0.wait()
+    lb1.wait()
+    lb2.wait()
+    for i in range(3):
+        tile_bias(braw.at[i], bt.at[i])
+    pl.semaphore_wait(barrier, heard)
+    for d in peers[:-1]:
+        remote(req.at[d], reqr.at[c], asem.at[0], asem.at[1], (r, d)).start()
+    asks = remote(
+        req.at[pl.ds(0, nc - 1)],
+        reqr.at[pl.ds(0, nc - 1)],
+        asem.at[0],
+        asem.at[1],
+        (r, peers[0]),
+    )
+    halos = []
+    for i, (src, dst, to, frm) in enumerate(
+        (
+            (crn.at[0], hc.at[0], 4, 7),
+            (crn.at[1], hc.at[1], 5, 6),
+            (crn.at[2], hc.at[2], 6, 5),
+            (crn.at[3], hc.at[3], 7, 4),
+            (edge.at[0:32], hy.at[0], 0, 1),
+            (edge.at[32:64], hy.at[1], 1, 0),
+            (vin.at[31], hx.at[0], 2, 3),
+            (vin.at[0], hx.at[1], 3, 2),
         )
-    ]
-    asks = [
-        send(req.at[d], reqr.at[c], qsend.at[k], qrecv.at[k], (r, d))
-        for k, d in enumerate(peers[:-1])
-    ]
+    ):
+        copy = remote(src, dst, hsend.at[i], hrecv.at[i], near[to][0])
+        start(copy, near[to][1])
+        halos.append((copy, near[to][1], near[frm][1]))
     reqr[c] = req[c]
 
     low16 = lanes((16, 128)) < 64
@@ -248,13 +297,13 @@
 
     lax.fori_loop(0, 2, coarse_conv, 0)
 
-    for copy in asks:
-        copy.wait_recv()
+    asks.wait_recv()
     i16 = sublanes((16, 128))
     l16 = lanes((16, 128))
     for k, d in enumerate(peers):
+        both = jnp.broadcast_to(reqr[d], (16, 128))
         for s in range(2):
-            cell = jnp.broadcast_to(reqr[d, s : s + 1, :], (16, 128))
+            cell = ((both >> (7 * s)) & 127) - 1
             px = (cell >> 3) * 4 + (i16 >> 2)
             py = ((cell >> 1) & 3) * 4 + (i16 & 3)
             target = jnp.where(cell >= 0, (px * 2 + (cell & 1)) * 16 + py, -1)
@@ -262,23 +311,21 @@
                 sel[k, s * 16 : (s + 1) * 16, j * 128 : (j + 1) * 128] = jnp.where(
                     target == l16 + j * 128, 1.0, 0.0
                 ).astype(BF)
-    for copy in halos:
-        copy.wait_recv()
-
-    for at, ok, i, row, j in ((0, r > 0, 0, 15, 0), (33, r < nr - 1, 1, 0, 2)):
-        corner_l = hc[j].astype(F32)[row : row + 1]
-        corner_r = hc[j + 1].astype(F32)[row : row + 1]
+    for copy, _, there in halos:
+        came(copy, there)
+
+    for at, ok, i, j in ((0, down, 0, 0), (33, up, 1, 2)):
         place(
             at,
             jnp.where(ok, hx[i].astype(F32), 0.0),
-            jnp.where(ok & (c > 0), corner_l, 0.0),
-            jnp.where(ok & (c < nc - 1), corner_r, 0.0),
+            jnp.where(ok & left, hc[j], 0.0),
+            jnp.where(ok & right, hc[j + 1], 0.0),
         )
     low32 = lanes((32, 128)) < 64
     x32 = sublanes((32, 256))
-    for i, ok in enumerate((c > 0, c < nc - 1)):
+    for i, ok in enumerate((left, right)):
         v = jnp.where(ok, hy[i].astype(F32), 0.0)
-        left = jnp.concatenate(
+        lhs = jnp.concatenate(
             [
                 jnp.concatenate([v[:, 0:256], jnp.where(low32, v[:, 256:384], 0.0)], axis=1),
                 jnp.concatenate([v[:, 256:512], jnp.where(low32, 0.0, v[:, 128:256])], axis=1),
@@ -286,7 +333,7 @@
             axis=0,
         ).astype(BF)
         part = [
-            jnp.dot(left, bw[0, 3 * dx + 2 * i], preferred_element_type=F32) for dx in range(3)
+            jnp.dot(lhs, bw[0, 3 * dx + 2 * i], preferred_element_type=F32) for dx in range(3)
         ]
         for g in range(2):
             before, here, after = [p[g * 32 : (g + 1) * 32] for p in part]
@@ -314,7 +361,6 @@
         return carry
 
     lax.fori_loop(0, X, coarse_out, 0, unroll=2)
-    gives = []
     for m in range(0, nc, 4):
         psend[m : m + 4] = (
             jnp.dot(
@@ -327,15 +373,23 @@
         )
         for k in range(m, m + 4):
             if k < nc - 1:
-                gives.append(
-                    send(psend.at[k], precv.at[c], asend.at[k], arecv.at[k], (r, peers[k]))
-                )
+                remote(
+                    psend.at[k], precv.at[c], gsem.at[0], gsem.at[1], (r, peers[k])
+                ).start()
+    gives = remote(
+        psend.at[pl.ds(0, nc - 1)],
+        precv.at[pl.ds(0, nc - 1)],
+        gsem.at[0],
+        gsem.at[1],
+        (r, peers[0]),
+    )
     precv[c] = psend[nc - 1]
-    loads[3].wait()
+    lw1.wait()
     build_weights(vw.at[1], bw.at[1])
-    loads[4].wait()
+    lw2.wait()
     build_weights(vw.at[2], bw.at[2])
-    loads[2].wait()
+    lfin.wait()
+    lnb.wait()
     b8 = sublanes((8, 128))
     low = lanes((8, 128)) < 64
     index, local, cross = [], [], []
@@ -368,17 +422,18 @@
 
     zero8 = jnp.zeros((8, 128), F32)
     blank = jnp.zeros((16, 384), BF)
-    for turn in range(2):
-        for i in range(10):
-            for j in range(10):
-                if i in (0, 9) or j in (0, 9):
-                    pad[turn, i, j] = blank
-    for copy in gives:
-        copy.wait_recv()
-    up = jnp.dot(sel2, precv[...].reshape(nc * 32, 256), preferred_element_type=F32)
+    for i in (0, 9):
+        for j in (0, 9):
+            pad[i, j] = blank
+    in_local = [jnp.concatenate([m] * 4, axis=1) for m in local[:4]]
+    in_cross = [jnp.concatenate([m] * 4, axis=1) for m in cross[:4]]
+    for copy, there, _ in halos:
+        sent(copy, there)
+    gives.wait_recv()
+    parents = jnp.dot(sel2, precv[...].reshape(nc * 32, 256), preferred_element_type=F32)
     grown = []
     for q in range(16):
-        u = up[q * 8 : (q + 1) * 8]
+        u = parents[q * 8 : (q + 1) * 8]
         parts = []
         for k in (0, 128):
             v = u[:, k : k + 128]
@@ -391,27 +446,22 @@
         v = vf[:, o : o + 512].astype(F32) + grown[(x // 2) * 4 + y // 2]
         s1[x, y] = jnp.concatenate([v[:, 0:256], v[:, 256:512]], axis=0).astype(BF)
 
-    def send_y(s, turn):
-        return [
-            send(s.at[:, 7], fr.at[turn, 2], fsend.at[turn, 2], frecv.at[turn, 2], (r, cpl)),
-            send(s.at[:, 0], fr.at[turn, 3], fsend.at[turn, 3], frecv.at[turn, 3], (r, cmi)),
-        ]
-
-    def send_x(s, turn):
-        return [
-            send(s.at[7], fr.at[turn, 0], fsend.at[turn, 0], frecv.at[turn, 0], (rp, c)),
-            send(s.at[0], fr.at[turn, 1], fsend.at[turn, 1], frecv.at[turn, 1], (rm, c)),
-        ]
+    def face(s, turn, f):
+        src = s.at[7 if f == 0 else 0] if f < 2 else s.at[:, 7 if f == 2 else 0]
+        to, frm = ((2, 3), (3, 2), (0, 1), (1, 0))[f]
+        copy = remote(src, fr.at[turn, f], hsend.at[f], frecv.at[turn, f], near[to][0])
+        start(copy, near[to][1])
+        return copy, near[to][1], near[frm][1]
 
     inside = range(1, 7)
     for x in range(8):
         begin(x, 0)
         begin(x, 7)
-    ymoves = send_y(s1, 0)
+    ymoves = [face(s1, 0, f) for f in (2, 3)]
     for y in inside:
         begin(0, y)
         begin(7, y)
-    moves = send_x(s1, 0) + ymoves
+    moves = [face(s1, 0, f) for f in (0, 1)] + ymoves
     for x in inside:
         for y in inside:
             begin(x, y)
@@ -422,7 +472,15 @@
                 v = load_cell(s, x, y)
                 zm = jnp.where(local[4], take(v[:, 384:512], index[4]), 0.0)
                 zp = jnp.where(local[5], take(v[:, 0:128], index[5]), 0.0)
-                pad[turn, x + 1, y + 1] = pack6(v, zm, zp, low)
+                pad[x + 1, y + 1] = pack6(v, zm, zp, low)
+            for f in range(4):
+                k = 7 if f % 2 == 0 else 0
+                v = load_cell(s, k, x) if f < 2 else load_cell(s, x, k)
+                v = pack6(jnp.where(in_local[f], take(v, index[f]), 0.0), zero8, zero8, low)
+                if f < 2:
+                    pad[9 * f, x + 1] = v
+                else:
+                    pad[x + 1, 9 * (f - 2)] = v
             return carry
 
         lax.fori_loop(0, 8, inner, 0)
@@ -432,7 +490,7 @@
             x0 = i * 4
             left = jnp.concatenate(
                 [
-                    pad[turn, pl.ds(x0 + dx, 4), dy : dy + 8].reshape(512, 384)
+                    pad[pl.ds(x0 + dx, 4), dy : dy + 8].reshape(512, 384)
                     for dx in range(3)
                     for dy in range(3)
                 ],
@@ -444,36 +502,33 @@
 
         lax.fori_loop(0, 2, conv, 0)
 
-    def fine_fix(s, turn, moves):
-        for f in range(4):
-            moves[f].wait_recv()
-            layer, at, tap = (7, 0, 0) if f % 2 == 0 else (0, 9, 2)
-            in_l = jnp.concatenate([local[f]] * 4, axis=1)
-            in_c = jnp.concatenate([cross[f]] * 4, axis=1)
-            for k in range(8):
-                near = load_cell(s, layer, k) if f < 2 else load_cell(s, k, layer)
-                far = load_cell(fr, turn, f, k)
-                v = jnp.where(
-                    in_l, take(near, index[f]), jnp.where(in_c, take(far, index[f]), 0.0)
+    def fine_fix(turn, moves):
+        for pair in ((0, 1), (2, 3)):
+            for f in pair:
+                came(moves[f][0], moves[f][2])
+            adds = []
+            for f in pair:
+                tap = 2 * (f % 2)
+                cells_of = [blank]
+                for k in range(8):
+                    v = load_cell(fr, turn, f, k)
+                    v = jnp.where(in_cross[f], take(v, index[f]), 0.0)
+                    cells_of.append(pack6(v, zero8, zero8, low))
+                cells_of.append(blank)
+                lhs = jnp.concatenate(
+                    [jnp.concatenate(cells_of[d : d + 8], axis=0) for d in range(3)], axis=1
                 )
-                v = pack6(v, zero8, zero8, low)
+                taps = [3 * tap + d if f < 2 else 3 * d + tap for d in range(3)]
+                rhs = jnp.concatenate([bw[turn + 1, k] for k in taps], axis=0)
+                adds.append(
+                    jnp.dot(lhs, rhs, preferred_element_type=F32).reshape(8, 16, 256)
+                )
+            for f, add in zip(pair, adds):
+                k = 7 * (f % 2)
                 if f < 2:
-                    pad[turn, at, k + 1] = v
+                    facc[k] = facc[k] + add
                 else:
-                    pad[turn, k + 1, at] = v
-            if f < 2:
-                left = [pad[turn, at, d : d + 8].reshape(128, 384) for d in range(3)]
-                right = bw[turn + 1, 3 * tap : 3 * tap + 3].reshape(1152, 256)
-            else:
-                left = [pad[turn, d : d + 8, at].reshape(128, 384) for d in range(3)]
-                right = jnp.concatenate([bw[turn + 1, 3 * d + tap] for d in range(3)], axis=0)
-            add = jnp.dot(
-                jnp.concatenate(left, axis=1), right, preferred_element_type=F32
-            ).reshape(8, 16, 256)
-            if f < 2:
-                facc[7 - layer] = facc[7 - layer] + add
-            else:
-                facc[:, 7 - layer] = facc[:, 7 - layer] + add
+                    facc[:, k] = facc[:, k] + add
 
     def keep(x, y):
         s2[x, y] = jnp.maximum(facc[x, y], 0.0).astype(BF)
@@ -493,33 +548,43 @@
 
     fine_main(s1, 0)
     each_inside(keep)
-    fine_fix(s1, 0, moves)
+    fine_fix(0, moves)
     for x in range(8):
         keep(x, 0)
         keep(x, 7)
-    ymoves = send_y(s2, 1)
+    for copy, there, _ in moves:
+        sent(copy, there)
+    ymoves = [face(s2, 1, f) for f in (2, 3)]
     for y in inside:
         keep(0, y)
         keep(7, y)
-    moves = send_x(s2, 1) + ymoves
+    moves = [face(s2, 1, f) for f in (0, 1)] + ymoves
     fine_main(s2, 1)
     each_inside(final)
-    fine_fix(s2, 1, moves)
+    fine_fix(1, moves)
     for x in range(8):
         final(x, 0)
         final(x, 7)
     for y in inside:
         final(0, y)
         final(7, y)
-    for copy in sends:
-        copy.wait_send()
+    for copy, there, _ in moves:
+        sent(copy, there)
+    asks.wait_send()
+    gives.wait_send()
 
 
 def put_out(coarse, fine, coarse_hbm, fine_hbm, sem):
-    copies = [
-        pltpu.make_async_copy(coarse, coarse_hbm, sem.at[0]),
-        pltpu.make_async_copy(fine, fine_hbm, sem.at[1]),
-    ]
+    copies = []
+    for k in range(PARTS):
+        n = X // PARTS
+        x = slice(k * n, (k + 1) * n)
+        copies.append(pltpu.make_async_copy(coarse.at[x], coarse_hbm.at[x], sem.at[2 * k]))
+        n = 32768 // PARTS
+        x = slice(k * n, (k + 1) * n)
+        copies.append(
+            pltpu.make_async_copy(fine.at[:, x], fine_hbm.at[:, x], sem.at[2 * k + 1])
+        )
     for copy in copies:
         copy.start()
     for copy in copies:
@@ -543,46 +608,46 @@
     nc = lax.axis_size("col")
     anywhere = pl.BlockSpec(memory_space=pl.ANY)
     vector = pl.BlockSpec(memory_space=pltpu.VMEM)
-    scalar = pl.BlockSpec(memory_space=pltpu.SMEM)
     dma = pltpu.SemaphoreType.DMA
     coarse, fine = pl.pallas_call(
         functools.partial(body, nr, nc),
         out_shape=(pltpu.VMEM(coarse_in.shape, BF), pltpu.VMEM(fine_in.shape, BF)),
-        in_specs=[anywhere, anywhere, vector, anywhere, anywhere, vector, anywhere, vector]
-        + [scalar] * 3,
+        in_specs=[anywhere] * 11,
         out_specs=(vector, vector),
         scratch_shapes=[
+            pltpu.SMEM((NB,), jnp.int32),
+            pltpu.SMEM((NB,), jnp.int32),
+            pltpu.SMEM((NB, 6), jnp.int32),
+            pltpu.VMEM((3, 1, CH), F32),
             pltpu.VMEM((X, Y, 512), BF),
             pltpu.VMEM((NB, 32768), BF),
             pltpu.VMEM((3, 27, CH, CH), BF),
             pltpu.VMEM((3, 9, 384, 256), BF),
             pltpu.VMEM((3, 1, 256), F32),
             pltpu.VMEM((64, 512), BF),
+            pltpu.VMEM((4, 1, 512), F32),
             pltpu.VMEM((2, 16, 512), BF),
             pltpu.VMEM((2, 32, 512), BF),
-            pltpu.VMEM((4, 16, 512), BF),
+            pltpu.VMEM((4, 1, 512), F32),
             pltpu.VMEM((2, 2, 32, 256), F32),
             pltpu.VMEM((34, 2, 16, 1152), BF),
             pltpu.VMEM((X, 2, 16, 256), F32),
             pltpu.VMEM((X, 2, 16, 256), BF),
-            pltpu.VMEM((nc, 8, 128), jnp.int32),
-            pltpu.VMEM((nc, 8, 128), jnp.int32),
+            pltpu.VMEM((nc, 1, 128), jnp.int32),
+            pltpu.VMEM((nc, 1, 128), jnp.int32),
             pltpu.VMEM((nc, 32, 1024), BF),
             pltpu.VMEM((nc, 32, 256), BF),
             pltpu.VMEM((nc, 32, 256), BF),
             pltpu.VMEM((8, 8, 16, 256), BF),
             pltpu.VMEM((8, 8, 16, 256), BF),
             pltpu.VMEM((2, 4, 8, 16, 256), BF),
-            pltpu.VMEM((2, 10, 10, 16, 384), BF),
+            pltpu.VMEM((10, 10, 16, 384), BF),
             pltpu.VMEM((8, 8, 16, 256), F32),
-            dma((5,)),
+            dma((11,)),
             dma((8,)),
             dma((8,)),
-            dma((nc,)),
-            dma((nc,)),
-            dma((nc,)),
-            dma((nc,)),
-            dma((2, 4)),
+            dma((2,)),
+            dma((2,)),
             dma((2, 4)),
         ],
         compiler_params=pltpu.CompilerParams(collective_id=0, has_side_effects=True),
@@ -607,7 +672,7 @@
         ),
         in_specs=[anywhere, anywhere],
         out_specs=(anywhere, anywhere),
-        scratch_shapes=[dma((2,))],
+        scratch_shapes=[dma((2 * PARTS,))],
         compiler_params=pltpu.CompilerParams(vmem_limit_bytes=1 << 20),
     )(coarse, fine)
 

time: 34.7 us -> 29.6 us (0.85); the launches traced: 34.1 us -> 29.5 us
  Pallas kernels: 33.5 us -> 28.8 us
    pallas_call x1, Pallas kernels: 32.5 us -> 27.9 us  [shards(): pl.pallas_call(functools.partial(body, nr, nc), out_shape=(pltpu.VMEM(coa...]
where the time goes in v2:
time: 29.6 us; the launch traced here: 29.5 us
  Pallas kernels  28.8 us (97%)
  between operations  0.64 us (2%)
    pallas_call x1, Pallas kernels, shards(): pl.pallas_call(functools.partial(body, nr, nc), out_shape=(pltpu.VMEM(coa...  27.9 us
    pallas_call x1, Pallas kernels, shards(): pl.pallas_call(put_out, out_shape=(jax.ShapeDtypeStruct(coarse_in.shape,...  1 us

profile of v2, /device:TPU:1, one launch (start us, length us, event | category | flops | bytes accessed | tf_op | source)
XLA Modules:
  0.0 29.5 jit_solution(5918652546534833202)
XLA Ops:
  0.6 27.9 %shard_map.122 = (bf16[32,16,512]{2,1,0:T(8,128)(2,1)S(1)}, bf16[8,32768]{1,0:T(8,128)(2,1)S(1)}) custom-call(bf16[32,16,512]{2,1,0:T(8,128)(2,1)} %cin.1, bf16[27,64,64]{2,1,0:T(8,128)(2,1)} %cw.1, f32[1,64]{1,0:T(1,128)} %bitcast.4, bf16[8,32768]{1,0:T(8,128)(2,1)} %fin.1, bf16[27,64,64]{2,1,0:T(8,128)(2,1)} %w1.1, f32[1,64]{1,0:T(1,128)} %bitcast.5, ...), custom_call_target="tpu_custom_call" | custom-call | tf_op jit(solution)/shard_map/pallas_call | solution.py:612
  28.5 1.0 %shard_map.123 = (bf16[32,16,512]{2,1,0:T(8,128)(2,1)}, bf16[8,32768]{1,0:T(8,128)(2,1)}) custom-call(bf16[32,16,512]{2,1,0:T(8,128)(2,1)S(1)} %get-tuple-element.4.coarse, bf16[8,32768]{1,0:T(8,128)(2,1)S(1)} %get-tuple-element.5.fine), custom_call_target="tpu_custom_call" | custom-call | tf_op jit(solution)/shard_map/pallas_call | solution.py:667

commit v3 on v2

--- a/solution.py
+++ b/solution.py
@@ -26,7 +26,6 @@
 
 def build_weights(w, bw):
     zero = jnp.zeros((64, 64), BF)
-    wide = jnp.zeros((64, 128), BF)
 
     def one(k, carry):
         wm, w0, wp = w[3 * k], w[3 * k + 1], w[3 * k + 2]
@@ -34,14 +33,50 @@
         b = jnp.concatenate([wp, w0], axis=1)
         c = jnp.concatenate([zero, wp], axis=1)
         d = jnp.concatenate([wm, zero], axis=1)
-        for r, (left, right) in enumerate(
-            ((a, wide), (b, d), (c, a), (wide, b), (wide, c), (d, wide))
-        ):
-            bw[k, r * 64 : (r + 1) * 64, 0:128] = left
-            bw[k, r * 64 : (r + 1) * 64, 128:256] = right
+        for r, v in enumerate((a, b, c)):
+            bw[k, r * 64 : (r + 1) * 64, 0:128] = v
+            bw[k, (r + 2) * 64 : (r + 3) * 64, 128:256] = v
+        bw[k, 320:384, 0:128] = d
+        bw[k, 64:128, 128:256] = d
         return carry
 
+    lax.fori_loop(0, 9, one, 0, unroll=9)
+
+
+def blank_weights(bw):
+    wide = jnp.zeros((64, 128), BF)
+
+    def one(k, carry):
+        for i in range(3):
+            for r, at in ((0, 128), (3, 0), (4, 0), (5, 128)):
+                bw[i, k, r * 64 : (r + 1) * 64, at : at + 128] = wide
+        return carry
+
     lax.fori_loop(0, 9, one, 0)
+
+
+def parent_weights(w, cu):
+    zero = jnp.zeros((64, 64), BF)
+    wide = jnp.zeros((64, 128), BF)
+    taps = {(0, 0): (0,), (0, 1): (1, 2), (1, 0): (0, 1), (1, 1): (2,)}
+    xs = {}
+    for key in taps:
+        for k in range(9):
+            xs[key, k] = sum(w[9 * d + k].astype(F32) for d in taps[key])
+    for px, tx in taps:
+        for py, ty in taps:
+            t = [
+                sum(xs[(px, tx), 3 * d + z] for d in taps[py, ty]) for z in range(3)
+            ]
+            a, b, d, e = [v.astype(BF) for v in (t[0], t[0] + t[1], t[1] + t[2], t[2])]
+            one = jnp.concatenate([d, b], axis=1)
+            two = jnp.concatenate([zero, e], axis=1)
+            three = jnp.concatenate([a, zero], axis=1)
+            for r, (left, right) in enumerate(
+                ((one, three), (two, one), (wide, two), (three, wide))
+            ):
+                cu[px, py, tx, ty, r * 64 : (r + 1) * 64, 0:128] = left
+                cu[px, py, tx, ty, r * 64 : (r + 1) * 64, 128:256] = right
 
 
 def tile_bias(b, bt):
@@ -62,6 +97,12 @@
 def pack6(v, zm, zp, low):
     first = jnp.concatenate([v[:, 0:256], jnp.where(low, v[:, 256:384], zm)], axis=1)
     second = jnp.concatenate([v[:, 256:512], jnp.where(low, zp, v[:, 128:256])], axis=1)
+    return jnp.concatenate([first, second], axis=0).astype(BF)
+
+
+def pack4(u, zm, zp, low):
+    first = jnp.concatenate([u[:, 0:128], jnp.where(low, u[:, 128:256], zm)], axis=1)
+    second = jnp.concatenate([u[:, 128:256], jnp.where(low, zp, u[:, 0:128])], axis=1)
     return jnp.concatenate([first, second], axis=0).astype(BF)
 
 
@@ -121,12 +162,18 @@
     fr,
     pad,
     facc,
+    cu,
+    ub,
+    fu,
+    pu,
     lsem,
     hsend,
     hrecv,
     asem,
     gsem,
+    fsend,
     frecv,
+    urecv,
 ):
     r = lax.axis_index("row")
     c = lax.axis_index("col")
@@ -197,6 +244,10 @@
         @pl.when(there)
         def _():
             copy.wait_recv()
+    ei = sublanes((64, 512))
+    ej = lanes((64, 512))
+    pick = jnp.where(ej == jnp.where(ei < 32, ei * 16 + 15, (ei - 32) * 16), 1.0, 0.0).astype(BF)
+    blank_weights(bw)
     ltile.wait()
     lcell.wait()
     tiles = [ptile[b] for b in range(NB)]
@@ -216,9 +267,6 @@
         req[t] = wanted[t : t + 1]
 
     lin.wait()
-    ei = sublanes((64, 512))
-    ej = lanes((64, 512))
-    pick = jnp.where(ej == jnp.where(ei < 32, ei * 16 + 15, (ei - 32) * 16), 1.0, 0.0).astype(BF)
     found = jnp.dot(pick, vin[...].reshape(512, 512), preferred_element_type=F32)
     edge[...] = found.astype(BF)
     for i, row in enumerate((31, 63, 0, 32)):
@@ -258,6 +306,28 @@
         halos.append((copy, near[to][1], near[frm][1]))
     reqr[c] = req[c]
 
+    def face(s, last, dst, ssem, rsem, f):
+        src = s.at[last if f == 0 else 0] if f < 2 else s.at[:, last if f == 2 else 0]
+        to, frm = ((2, 3), (3, 2), (0, 1), (1, 0))[f]
+        copy = remote(src, dst.at[f], ssem.at[f], rsem.at[f], near[to][0])
+        start(copy, near[to][1])
+        return copy, near[to][1], near[frm][1]
+
+    def begin(x, y):
+        o = (x * 8 + y) * 512
+        v = vf[:, o : o + 512].astype(F32)
+        s1[x, y] = jnp.concatenate([v[:, 0:256], v[:, 256:512]], axis=0).astype(BF)
+
+    inside = range(1, 7)
+    lfin.wait()
+    for x in range(8):
+        begin(x, 0)
+        begin(x, 7)
+    for y in inside:
+        begin(0, y)
+        begin(7, y)
+    moves = [face(s1, 7, fr.at[0], fsend, frecv.at[0], f) for f in range(4)]
+
     low16 = lanes((16, 128)) < 64
     zero16 = jnp.zeros((16, 128), F32)
     y16 = sublanes((16, 512))
@@ -296,21 +366,6 @@
         return carry
 
     lax.fori_loop(0, 2, coarse_conv, 0)
-
-    asks.wait_recv()
-    i16 = sublanes((16, 128))
-    l16 = lanes((16, 128))
-    for k, d in enumerate(peers):
-        both = jnp.broadcast_to(reqr[d], (16, 128))
-        for s in range(2):
-            cell = ((both >> (7 * s)) & 127) - 1
-            px = (cell >> 3) * 4 + (i16 >> 2)
-            py = ((cell >> 1) & 3) * 4 + (i16 & 3)
-            target = jnp.where(cell >= 0, (px * 2 + (cell & 1)) * 16 + py, -1)
-            for j in range(8):
-                sel[k, s * 16 : (s + 1) * 16, j * 128 : (j + 1) * 128] = jnp.where(
-                    target == l16 + j * 128, 1.0, 0.0
-                ).astype(BF)
     for copy, _, there in halos:
         came(copy, there)
 
@@ -361,7 +416,24 @@
         return carry
 
     lax.fori_loop(0, X, coarse_out, 0, unroll=2)
+
+    asks.wait_recv()
+    i16 = sublanes((16, 128))
+    l16 = lanes((16, 128))
+    def choose(k, d):
+        both = jnp.broadcast_to(reqr[d], (16, 128))
+        for s in range(2):
+            cell = ((both >> (7 * s)) & 127) - 1
+            px = (cell >> 3) * 4 + (i16 >> 2)
+            py = ((cell >> 1) & 3) * 4 + (i16 & 3)
+            target = jnp.where(cell >= 0, (px * 2 + (cell & 1)) * 16 + py, -1)
+            for j in range(8):
+                sel[k, s * 16 : (s + 1) * 16, j * 128 : (j + 1) * 128] = jnp.where(
+                    target == l16 + j * 128, 1.0, 0.0
+                ).astype(BF)
     for m in range(0, nc, 4):
+        for k in range(m, m + 4):
+            choose(k, peers[k])
         psend[m : m + 4] = (
             jnp.dot(
                 sel[m : m + 4].reshape(128, 1024),
@@ -387,8 +459,6 @@
     lw1.wait()
     build_weights(vw.at[1], bw.at[1])
     lw2.wait()
-    build_weights(vw.at[2], bw.at[2])
-    lfin.wait()
     lnb.wait()
     b8 = sublanes((8, 128))
     low = lanes((8, 128)) < 64
@@ -429,42 +499,6 @@
     in_cross = [jnp.concatenate([m] * 4, axis=1) for m in cross[:4]]
     for copy, there, _ in halos:
         sent(copy, there)
-    gives.wait_recv()
-    parents = jnp.dot(sel2, precv[...].reshape(nc * 32, 256), preferred_element_type=F32)
-    grown = []
-    for q in range(16):
-        u = parents[q * 8 : (q + 1) * 8]
-        parts = []
-        for k in (0, 128):
-            v = u[:, k : k + 128]
-            w = pltpu.roll(v, 64, 1)
-            parts += [jnp.where(low, v, w), jnp.where(low, w, v)]
-        grown.append(jnp.concatenate(parts, axis=1))
-
-    def begin(x, y):
-        o = (x * 8 + y) * 512
-        v = vf[:, o : o + 512].astype(F32) + grown[(x // 2) * 4 + y // 2]
-        s1[x, y] = jnp.concatenate([v[:, 0:256], v[:, 256:512]], axis=0).astype(BF)
-
-    def face(s, turn, f):
-        src = s.at[7 if f == 0 else 0] if f < 2 else s.at[:, 7 if f == 2 else 0]
-        to, frm = ((2, 3), (3, 2), (0, 1), (1, 0))[f]
-        copy = remote(src, fr.at[turn, f], hsend.at[f], frecv.at[turn, f], near[to][0])
-        start(copy, near[to][1])
-        return copy, near[to][1], near[frm][1]
-
-    inside = range(1, 7)
-    for x in range(8):
-        begin(x, 0)
-        begin(x, 7)
-    ymoves = [face(s1, 0, f) for f in (2, 3)]
-    for y in inside:
-        begin(0, y)
-        begin(7, y)
-    moves = [face(s1, 0, f) for f in (0, 1)] + ymoves
-    for x in inside:
-        for y in inside:
-            begin(x, y)
 
     def fine_main(s, turn):
         def inner(x, carry):
@@ -497,7 +531,7 @@
                 axis=1,
             )
             out = jnp.dot(left, bw[turn + 1].reshape(3456, 256), preferred_element_type=F32)
-            facc[pl.ds(x0, 4)] = (out + bias).reshape(4, 8, 16, 256)
+            facc[pl.ds(i * 2, 2)] = (out + bias).reshape(2, 2, 4, 2, 16, 256)
             return carry
 
         lax.fori_loop(0, 2, conv, 0)
@@ -524,43 +558,117 @@
                     jnp.dot(lhs, rhs, preferred_element_type=F32).reshape(8, 16, 256)
                 )
             for f, add in zip(pair, adds):
-                k = 7 * (f % 2)
+                k, h = 3 * (f % 2), f % 2
                 if f < 2:
-                    facc[k] = facc[k] + add
+                    facc[k, h] = facc[k, h] + add.reshape(4, 2, 16, 256)
                 else:
-                    facc[:, k] = facc[:, k] + add
+                    facc[:, :, k, h] = facc[:, :, k, h] + add.reshape(4, 2, 16, 256)
+
+    def add_to(x, y):
+        return facc[x // 2, x % 2, y // 2, y % 2]
 
     def keep(x, y):
-        s2[x, y] = jnp.maximum(facc[x, y], 0.0).astype(BF)
+        s2[x, y] = jnp.maximum(add_to(x, y), 0.0).astype(BF)
 
     def final(x, y):
-        v = jnp.maximum(facc[x, y], 0.0)
-        at = pl.multiple_of((x * 8 + y) * 512, 512)
-        fout[:, pl.ds(at, 512)] = jnp.concatenate([v[0:8], v[8:16]], axis=1).astype(BF)
-
-    def each_inside(put):
-        def one(x, carry):
-            for y in inside:
-                put(x, y)
-            return carry
-
-        lax.fori_loop(1, 7, one, 0)
-
+        v = jnp.maximum(add_to(x, y), 0.0)
+        fout[:, (x * 8 + y) * 512 : (x * 8 + y + 1) * 512] = jnp.concatenate(
+            [v[0:8], v[8:16]], axis=1
+        ).astype(BF)
+
+    for x in inside:
+        for y in inside:
+            begin(x, y)
     fine_main(s1, 0)
-    each_inside(keep)
+    parent_weights(vw.at[1], cu)
     fine_fix(0, moves)
+    gives.wait_recv()
+    parents = jnp.dot(sel2, precv[...].reshape(nc * 32, 256), preferred_element_type=F32)
+    grown = [parents[q * 8 : (q + 1) * 8] for q in range(16)]
+    for q in range(16):
+        u = grown[q]
+        ub[q // 4, q % 4] = jnp.concatenate([u[:, 0:128], u[:, 128:256]], axis=0).astype(BF)
+    umoves = [face(ub, 3, fu, hsend, urecv, f) for f in range(4)]
+
+    for q in range(16):
+        u = grown[q]
+        zm = jnp.where(local[4], take(u[:, 128:256], index[4]), 0.0)
+        zp = jnp.where(local[5], take(u[:, 0:128], index[5]), 0.0)
+        pu[q // 4 + 1, q % 4 + 1] = pack4(u, zm, zp, low)
+    ublank = jnp.zeros((16, 256), BF)
+    for i in (0, 5):
+        for j in (0, 5):
+            pu[i, j] = ublank
+    for k in range(4):
+        for f in range(4):
+            at = 3 * (1 - f % 2)
+            u = grown[at * 4 + k] if f < 2 else grown[k * 4 + at]
+            half = in_local[f][:, 0:256]
+            v = pack4(jnp.where(half, take(u, index[f]), 0.0), zero8, zero8, low)
+            if f < 2:
+                pu[5 * f, k + 1] = v
+            else:
+                pu[k + 1, 5 * (f - 2)] = v
+    for px in range(2):
+        for py in range(2):
+            lhs = jnp.concatenate(
+                [
+                    pu[px + tx : px + tx + 4, py + ty : py + ty + 4].reshape(256, 256)
+                    for tx in range(2)
+                    for ty in range(2)
+                ],
+                axis=1,
+            )
+            out = jnp.dot(lhs, cu[px, py].reshape(1024, 256), preferred_element_type=F32)
+            facc[:, px, :, py] = facc[:, px, :, py] + out.reshape(4, 4, 16, 256)
+    build_weights(vw.at[2], bw.at[2])
+    for pair in ((0, 1), (2, 3)):
+        for f in pair:
+            came(umoves[f][0], umoves[f][2])
+        adds = []
+        for f in pair:
+            tap = f % 2
+            strip = [ublank]
+            for k in range(4):
+                v = fu[f, k].astype(F32)
+                u = jnp.concatenate([v[0:8], v[8:16]], axis=1)
+                u = jnp.where(in_cross[f][:, 0:256], take(u, index[f]), 0.0)
+                strip.append(pack4(u, zero8, zero8, low))
+            strip.append(ublank)
+            for p in range(2):
+                lhs = jnp.concatenate(
+                    [jnp.concatenate(strip[p + t : p + t + 4], axis=0) for t in range(2)],
+                    axis=1,
+                )
+                if f < 2:
+                    rhs = cu[tap, p, tap].reshape(512, 256)
+                else:
+                    rhs = jnp.concatenate([cu[p, tap, t, tap] for t in range(2)], axis=0)
+                add = jnp.dot(lhs, rhs, preferred_element_type=F32).reshape(4, 16, 256)
+                adds.append((f, p, add))
+        for f, p, add in adds:
+            e, tap = 3 * (f % 2), f % 2
+            if f < 2:
+                facc[e, tap, :, p] = facc[e, tap, :, p] + add
+            else:
+                facc[:, p, e, tap] = facc[:, p, e, tap] + add
     for x in range(8):
         keep(x, 0)
         keep(x, 7)
-    for copy, there, _ in moves:
-        sent(copy, there)
-    ymoves = [face(s2, 1, f) for f in (2, 3)]
     for y in inside:
         keep(0, y)
         keep(7, y)
-    moves = [face(s2, 1, f) for f in (0, 1)] + ymoves
+    for copy, there, _ in moves:
+        sent(copy, there)
+    moves = [face(s2, 7, fr.at[1], fsend, frecv.at[1], f) for f in (2, 3, 0, 1)]
+    moves = moves[2:] + moves[:2]
+    for x in inside:
+        for y in inside:
+            keep(x, y)
     fine_main(s2, 1)
-    each_inside(final)
+    for x in inside:
+        for y in inside:
+            final(x, y)
     fine_fix(1, moves)
     for x in range(8):
         final(x, 0)
@@ -568,7 +676,7 @@
     for y in inside:
         final(0, y)
         final(7, y)
-    for copy, there, _ in moves:
+    for copy, there, _ in moves + umoves:
         sent(copy, there)
     asks.wait_send()
     gives.wait_send()
@@ -642,13 +750,19 @@
             pltpu.VMEM((8, 8, 16, 256), BF),
             pltpu.VMEM((2, 4, 8, 16, 256), BF),
             pltpu.VMEM((10, 10, 16, 384), BF),
-            pltpu.VMEM((8, 8, 16, 256), F32),
+            pltpu.VMEM((4, 2, 4, 2, 16, 256), F32),
+            pltpu.VMEM((2, 2, 2, 2, 256, 256), BF),
+            pltpu.VMEM((4, 4, 16, 128), BF),
+            pltpu.VMEM((4, 4, 16, 128), BF),
+            pltpu.VMEM((6, 6, 16, 256), BF),
             dma((11,)),
             dma((8,)),
             dma((8,)),
             dma((2,)),
             dma((2,)),
+            dma((4,)),
             dma((2, 4)),
+            dma((4,)),
         ],
         compiler_params=pltpu.CompilerParams(collective_id=0, has_side_effects=True),
     )(

time: 29.6 us -> 28.6 us (0.966)
  Pallas kernels: 28.8 us -> 27.6 us
    pallas_call x1, Pallas kernels: 27.9 us -> 26.6 us  [shards(): pl.pallas_call(functools.partial(body, nr, nc), out_shape=(pltpu.VMEM(coa...]
where the time goes in v3:
time: 28.6 us; the launch traced here: 28.2 us
  Pallas kernels  27.6 us (97%)
  between operations  0.64 us (2%)
    pallas_call x1, Pallas kernels, shards(): pl.pallas_call(functools.partial(body, nr, nc), out_shape=(pltpu.VMEM(coa...  26.6 us
    pallas_call x1, Pallas kernels, shards(): pl.pallas_call(put_out, out_shape=(jax.ShapeDtypeStruct(coarse_in.shape,...  1 us

profile of v3, /device:TPU:1, one launch (start us, length us, event | category | flops | bytes accessed | tf_op | source)
XLA Modules:
  0.0 28.2 jit_solution(9160886452739612760)
XLA Ops:
  0.6 26.6 %shard_map.122 = (bf16[32,16,512]{2,1,0:T(8,128)(2,1)S(1)}, bf16[8,32768]{1,0:T(8,128)(2,1)S(1)}) custom-call(bf16[32,16,512]{2,1,0:T(8,128)(2,1)} %cin.1, bf16[27,64,64]{2,1,0:T(8,128)(2,1)} %cw.1, f32[1,64]{1,0:T(1,128)} %bitcast.4, bf16[8,32768]{1,0:T(8,128)(2,1)} %fin.1, bf16[27,64,64]{2,1,0:T(8,128)(2,1)} %w1.1, f32[1,64]{1,0:T(1,128)} %bitcast.5, ...), custom_call_target="tpu_custom_call" | custom-call | tf_op jit(solution)/shard_map/pallas_call | solution.py:720
  27.2 1.0 %shard_map.123 = (bf16[32,16,512]{2,1,0:T(8,128)(2,1)}, bf16[8,32768]{1,0:T(8,128)(2,1)}) custom-call(bf16[32,16,512]{2,1,0:T(8,128)(2,1)S(1)} %get-tuple-element.4.coarse, bf16[8,32768]{1,0:T(8,128)(2,1)S(1)} %get-tuple-element.5.fine), custom_call_target="tpu_custom_call" | custom-call | tf_op jit(solution)/shard_map/pallas_call | solution.py:781

commit v4 on v3

--- a/solution.py
+++ b/solution.py
@@ -500,6 +500,17 @@
     for copy, there, _ in halos:
         sent(copy, there)
 
+    def by_parity(one):
+        @pl.when(lax.rem(r, 2) == 0)
+        def _():
+            one((0, 1))
+
+        one((2, 3))
+
+        @pl.when(lax.rem(r, 2) == 1)
+        def _():
+            one((0, 1))
+
     def fine_main(s, turn):
         def inner(x, carry):
             for y in range(8):
@@ -537,7 +548,7 @@
         lax.fori_loop(0, 2, conv, 0)
 
     def fine_fix(turn, moves):
-        for pair in ((0, 1), (2, 3)):
+        def one(pair):
             for f in pair:
                 came(moves[f][0], moves[f][2])
             adds = []
@@ -563,6 +574,8 @@
                     facc[k, h] = facc[k, h] + add.reshape(4, 2, 16, 256)
                 else:
                     facc[:, :, k, h] = facc[:, :, k, h] + add.reshape(4, 2, 16, 256)
+
+        by_parity(one)
 
     def add_to(x, y):
         return facc[x // 2, x % 2, y // 2, y % 2]
@@ -622,7 +635,7 @@
             out = jnp.dot(lhs, cu[px, py].reshape(1024, 256), preferred_element_type=F32)
             facc[:, px, :, py] = facc[:, px, :, py] + out.reshape(4, 4, 16, 256)
     build_weights(vw.at[2], bw.at[2])
-    for pair in ((0, 1), (2, 3)):
+    def up_fix(pair):
         for f in pair:
             came(umoves[f][0], umoves[f][2])
         adds = []
@@ -652,6 +665,8 @@
                 facc[e, tap, :, p] = facc[e, tap, :, p] + add
             else:
                 facc[:, p, e, tap] = facc[:, p, e, tap] + add
+
+    by_parity(up_fix)
     for x in range(8):
         keep(x, 0)
         keep(x, 7)

time: 28.6 us -> 27.9 us (0.976)
  Pallas kernels: 27.6 us -> 26.9 us
    pallas_call x1, Pallas kernels: 26.6 us -> 25.9 us  [shards(): pl.pallas_call(functools.partial(body, nr, nc), out_shape=(pltpu.VMEM(coa...]
where the time goes in v4:
time: 27.9 us; the launch traced here: 27.5 us
  Pallas kernels  26.9 us (96%)
  between operations  0.64 us (2%)
    pallas_call x1, Pallas kernels, shards(): pl.pallas_call(functools.partial(body, nr, nc), out_shape=(pltpu.VMEM(coa...  25.9 us
    pallas_call x1, Pallas kernels, shards(): pl.pallas_call(put_out, out_shape=(jax.ShapeDtypeStruct(coarse_in.shape,...  1 us

profile of v4, /device:TPU:1, one launch (start us, length us, event | category | flops | bytes accessed | tf_op | source)
XLA Modules:
  0.0 27.5 jit_solution(1062221385943246865)
XLA Ops:
  0.6 25.9 %shard_map.122 = (bf16[32,16,512]{2,1,0:T(8,128)(2,1)S(1)}, bf16[8,32768]{1,0:T(8,128)(2,1)S(1)}) custom-call(bf16[32,16,512]{2,1,0:T(8,128)(2,1)} %cin.1, bf16[27,64,64]{2,1,0:T(8,128)(2,1)} %cw.1, f32[1,64]{1,0:T(1,128)} %bitcast.4, bf16[8,32768]{1,0:T(8,128)(2,1)} %fin.1, bf16[27,64,64]{2,1,0:T(8,128)(2,1)} %w1.1, f32[1,64]{1,0:T(1,128)} %bitcast.5, ...), custom_call_target="tpu_custom_call" | custom-call | tf_op jit(solution)/shard_map/pallas_call | solution.py:735
  26.5 1.0 %shard_map.123 = (bf16[32,16,512]{2,1,0:T(8,128)(2,1)}, bf16[8,32768]{1,0:T(8,128)(2,1)}) custom-call(bf16[32,16,512]{2,1,0:T(8,128)(2,1)S(1)} %get-tuple-element.4.coarse, bf16[8,32768]{1,0:T(8,128)(2,1)S(1)} %get-tuple-element.5.fine), custom_call_target="tpu_custom_call" | custom-call | tf_op jit(solution)/shard_map/pallas_call | solution.py:796

commit v5 on v4

--- a/solution.py
+++ b/solution.py
@@ -10,6 +10,7 @@
 X = 32
 Y = 16
 NB = 8
+CHUNKS = (2, 6, 8)
 PARTS = 2
 F32 = jnp.float32
 BF = jnp.bfloat16
@@ -431,23 +432,25 @@
                 sel[k, s * 16 : (s + 1) * 16, j * 128 : (j + 1) * 128] = jnp.where(
                     target == l16 + j * 128, 1.0, 0.0
                 ).astype(BF)
-    for m in range(0, nc, 4):
-        for k in range(m, m + 4):
+    m = 0
+    for n in CHUNKS if nc == 16 else (nc,):
+        for k in range(m, m + n):
             choose(k, peers[k])
-        psend[m : m + 4] = (
+        psend[m : m + n] = (
             jnp.dot(
-                sel[m : m + 4].reshape(128, 1024),
+                sel[m : m + n].reshape(n * 32, 1024),
                 cs[...].reshape(1024, 256),
                 preferred_element_type=F32,
             )
             .astype(BF)
-            .reshape(4, 32, 256)
+            .reshape(n, 32, 256)
         )
-        for k in range(m, m + 4):
+        for k in range(m, m + n):
             if k < nc - 1:
                 remote(
                     psend.at[k], precv.at[c], gsem.at[0], gsem.at[1], (r, peers[k])
                 ).start()
+        m += n
     gives = remote(
         psend.at[pl.ds(0, nc - 1)],
         precv.at[pl.ds(0, nc - 1)],
@@ -595,6 +598,8 @@
     fine_main(s1, 0)
     parent_weights(vw.at[1], cu)
     fine_fix(0, moves)
+
+    build_weights(vw.at[2], bw.at[2])
     gives.wait_recv()
     parents = jnp.dot(sel2, precv[...].reshape(nc * 32, 256), preferred_element_type=F32)
     grown = [parents[q * 8 : (q + 1) * 8] for q in range(16)]
@@ -634,7 +639,7 @@
             )
             out = jnp.dot(lhs, cu[px, py].reshape(1024, 256), preferred_element_type=F32)
             facc[:, px, :, py] = facc[:, px, :, py] + out.reshape(4, 4, 16, 256)
-    build_weights(vw.at[2], bw.at[2])
+
     def up_fix(pair):
         for f in pair:
             came(umoves[f][0], umoves[f][2])

time: 27.9 us -> 27.9 us (level)
  no operation moved by 1% of the time
where the time goes in v5:
time: 27.9 us; the launch traced here: 27.5 us
  Pallas kernels  26.9 us (96%)
  between operations  0.64 us (2%)
    pallas_call x1, Pallas kernels, shards(): pl.pallas_call(functools.partial(body, nr, nc), out_shape=(pltpu.VMEM(coa...  25.9 us
    pallas_call x1, Pallas kernels, shards(): pl.pallas_call(put_out, out_shape=(jax.ShapeDtypeStruct(coarse_in.shape,...  1 us

profile of v5, /device:TPU:1, one launch (start us, length us, event | category | flops | bytes accessed | tf_op | source)
XLA Modules:
  0.0 27.5 jit_solution(14483223774920876700)
XLA Ops:
  0.6 25.9 %shard_map.122 = (bf16[32,16,512]{2,1,0:T(8,128)(2,1)S(1)}, bf16[8,32768]{1,0:T(8,128)(2,1)S(1)}) custom-call(bf16[32,16,512]{2,1,0:T(8,128)(2,1)} %cin.1, bf16[27,64,64]{2,1,0:T(8,128)(2,1)} %cw.1, f32[1,64]{1,0:T(1,128)} %bitcast.4, bf16[8,32768]{1,0:T(8,128)(2,1)} %fin.1, bf16[27,64,64]{2,1,0:T(8,128)(2,1)} %w1.1, f32[1,64]{1,0:T(1,128)} %bitcast.5, ...), custom_call_target="tpu_custom_call" | custom-call | tf_op jit(solution)/shard_map/pallas_call | solution.py:740
  26.5 1.0 %shard_map.123 = (bf16[32,16,512]{2,1,0:T(8,128)(2,1)}, bf16[8,32768]{1,0:T(8,128)(2,1)}) custom-call(bf16[32,16,512]{2,1,0:T(8,128)(2,1)S(1)} %get-tuple-element.4.coarse, bf16[8,32768]{1,0:T(8,128)(2,1)S(1)} %get-tuple-element.5.fine), custom_call_target="tpu_custom_call" | custom-call | tf_op jit(solution)/shard_map/pallas_call | solution.py:801
